TPU v7x, 256 devices: a whole 4x4x8 slice. The times are simulated.
256 devices in a mesh: ex: 2 (over core), slab: 128 (over z, y, x).
Axes of the slice: x: 4, y: 4, z: 8, core: 2. Of those that a mesh axis runs over, the one named last changes fastest.
Arguments:
- volume: bfloat16 [2, 16, 128, 32, 128], P('ex', None, 'slab'), may hold values from -6 to 6
- cotangent: bfloat16 [2, 16, 128, 32, 128], P('ex', None, 'slab')
- gate_mask: int32 [2, 2, 128, 32, 128], P('ex', None, 'slab'), may hold values 0 or 1
- loss_scale: float32 [2], P('ex'), may hold values from 0.05 to 5
- canary: int32 [2], P('ex'), may hold values from 0 to 15
- kernels: bfloat16 [2, 32, 432], replicated, may hold values from -0.3125 to 0.3125
Outputs:
- input_grad: float32 [2, 16, 128, 32, 128], P('ex', None, 'slab')
- kernel_grad: float32 [2, 32, 432], replicated
All inputs are finite; a program needn't handle non-finite values. No bound on the sum of `gate_mask` on one device may be relied on, other than what follows from the above.
Results may differ from a plain program's by a relative error of at most 0.0037.
Values may be sent and summed in bfloat16 or wider, within the bound.
A program may use at most 64 MiB of HBM per device.

v0:
```python
import jax
import jax.numpy as jnp
from jax import lax
from jax.sharding import PartitionSpec as P


def with_halo(array, sides, width):
    for axis, dim in sides:
        peers, length = (lax.axis_size(axis), array.shape[dim])
        up = [(i, (i + 1) % peers) for i in range(peers - 1)]
        down = [(j, i) for i, j in up]
        last = lax.slice_in_dim(array, length - width, length, axis=dim)
        leading = lax.slice_in_dim(array, 0, width, axis=dim)
        before = lax.ppermute(last, axis, up)
        after = lax.ppermute(leading, axis, down)
        array = jnp.concatenate([before, array, after], axis=dim)
    return array


def columns(extended):
    zs = extended.shape[2] - 2
    hs, ws = (extended.shape[3], extended.shape[4])
    padded = jnp.pad(extended, ((0, 0), (0, 0), (0, 0), (1, 1), (1, 1)))
    taps = []
    for dz in range(3):
        for dh in range(3):
            for dw in range(3):
                taps.append(padded[:, :, dz : dz + zs, dh : dh + hs, dw : dw + ws])
    stacked = jnp.stack(taps, axis=1)
    return stacked.reshape((extended.shape[0], 27 * extended.shape[1], zs, hs, ws))


def back_columns(extended):
    zs = extended.shape[2] - 2
    hs, ws = (extended.shape[3], extended.shape[4])
    padded = jnp.pad(extended, ((0, 0), (0, 0), (0, 0), (1, 1), (1, 1)))
    taps = []
    for dz in range(3):
        for dh in range(3):
            for dw in range(3):
                taps.append(
                    padded[:, :, 2 - dz : 2 - dz + zs, 2 - dh : 2 - dh + hs, 2 - dw : 2 - dw + ws]
                )
    return jnp.stack(taps, axis=1)


def layer_forward(field, kernel):
    extended = with_halo(field, (("slab", 2),), 1)
    patches = columns(extended)
    pre = jnp.einsum("ok,ekzhw->eozhw", kernel, patches, preferred_element_type=jnp.float32)
    return (pre, patches)


def layer_backward(delta, kernel, patches):
    grads = jnp.einsum("eozhw,ekzhw->eok", delta, patches, preferred_element_type=jnp.float32)
    extended = with_halo(delta, (("slab", 2),), 1)
    width = kernel.shape[1] // 27
    shaped = kernel.reshape((kernel.shape[0], 27, width))
    spread = jnp.einsum(
        "otc,etozhw->eczhw", shaped, back_columns(extended), preferred_element_type=jnp.float32
    )
    return (grads, spread)


def per_device(volume, cotangent, gate_mask, loss_scale, canary, kernels):
    chans = volume.shape[1]
    local_ex = volume.shape[0]
    mask_one = gate_mask[:, 0][:, None].astype(jnp.float32)
    mask_two = gate_mask[:, 1][:, None].astype(jnp.float32)
    pre_one, patches_one = layer_forward(volume, kernels[0])
    value_one = pre_one[:, :chans]
    sig_one = jax.nn.sigmoid(pre_one[:, chans:])
    hidden = (volume.astype(jnp.float32) + value_one * sig_one * mask_one).astype(jnp.bfloat16)
    pre_two, patches_two = layer_forward(hidden, kernels[1])
    value_two = pre_two[:, :chans]
    sig_two = jax.nn.sigmoid(pre_two[:, chans:])
    channel_ids = jnp.arange(chans, dtype=jnp.int32)
    weights = 1.0 + 2.0 * (channel_ids[None, :] == canary[:, None]).astype(jnp.float32)
    weights = weights * loss_scale[:, None]
    grad_out = cotangent.astype(jnp.float32) * weights[:, :, None, None, None]
    delta_two = jnp.concatenate(
        [
            grad_out * sig_two * mask_two,
            grad_out * value_two * sig_two * (1.0 - sig_two) * mask_two,
        ],
        axis=1,
    ).astype(jnp.bfloat16)
    grad_two, spread_two = layer_backward(delta_two, kernels[1], patches_two)
    grad_hidden = grad_out + spread_two
    delta_one = jnp.concatenate(
        [
            grad_hidden * sig_one * mask_one,
            grad_hidden * value_one * sig_one * (1.0 - sig_one) * mask_one,
        ],
        axis=1,
    ).astype(jnp.bfloat16)
    grad_one, spread_one = layer_backward(delta_one, kernels[0], patches_one)
    input_grad = grad_hidden + spread_one
    stacked = jnp.stack([grad_one, grad_two], axis=1)
    flat = stacked.reshape((local_ex, -1))
    depth = volume.shape[2] * lax.axis_size("slab")
    bound = 20.0 * jnp.sqrt(jnp.float32(depth * volume.shape[3] * volume.shape[4]))
    examples = local_ex * lax.axis_size("ex")
    scaling = jnp.sqrt(jnp.float32(108 * chans * chans)) / (bound * jnp.sqrt(jnp.float32(examples)))
    summed = lax.psum(flat, "slab")
    norm = jnp.sqrt(jnp.sum(summed * summed, axis=1) + 1e-06)
    factor = jnp.minimum(1.0, bound / norm)
    local_total = jnp.sum(summed * factor[:, None], axis=0)
    total = lax.psum(local_total, "ex")
    kernel_grad = (total * scaling).reshape(kernels.shape)
    return (input_grad, kernel_grad)


def solution(mesh):
    placed = (
        P("ex", None, "slab", None, None),
        P("ex", None, "slab", None, None),
        P("ex", None, "slab", None, None),
        P("ex"),
        P("ex"),
        P(),
    )
    return jax.shard_map(
        per_device,
        mesh=mesh,
        in_specs=placed,
        out_specs=(P("ex", None, "slab", None, None), P()),
        check_vma=False,
    )
```

profile of v0, /device:TPU:1, one launch (start us, length us, event | category | flops | bytes accessed | tf_op | source)
XLA Modules:
  0.0 345.2 jit_solution(6189408591076951782)
XLA Ops:
  7.2 1.3 collective-permute-start.1
  8.5 4.6 %collective-permute-start = (bf16[1,16,1,32,128]{4,3,1,2,0:T(8,128)(2,1)}, bf16[1,16,1,32,128]{4,3,1,2,0:T(8,128)(2,1)S(1)}, u32[]{:S(2)}, u32[]{:S(2)}) collective-permute-start(bf16[1,16,1,32,128]{4,3,1,2,0:T(8,128)(2,1)} %bitcast.510), channel_id=1, source_target_pairs={{0,1},{1,2},{2,3},{3,4},{4,5},{5,6},{6,7},{7,8},{8,9},{9,10},{10,1... | collective-permute-start | bytes 393224 | tf_op jit(solution)/shard_map/ppermute | solution.py:14
  13.1 1.3 convert_bitcast_fusion
  14.4 0.9 collective-permute-done
  15.3 1.6 select_maximum_fusion.5
  19.8 1.4 copy.24
  23.5 1.3 collective-permute-start.3
  24.8 5.0 %collective-permute-start.2 = (bf16[1,16,1,32,128]{4,1,3,2,0:T(8,128)(2,1)}, bf16[1,16,1,32,128]{4,1,3,2,0:T(8,128)(2,1)}, u32[]{:S(2)}, u32[]{:S(2)}) collective-permute-start(bf16[1,16,1,32,128]{4,1,3,2,0:T(8,128)(2,1)} %add_convert_fusion), channel_id=1, source_target_pairs={{0,1},{1,2},{2,3},{3,4},{4,5},{5,6},{6,7},{7,8},{8,9},{9,10},{10,1... | collective-permute-start | bytes 393224 | tf_op jit(solution)/shard_map/ppermute | solution.py:14
  31.7 1.5 copy.27
  33.2 1.4 select_maximum_fusion.7
  35.0 0.9 constant_dynamic-update-slice_fusion.49
  36.7 0.9 constant_dynamic-update-slice_fusion.40
  38.4 0.9 constant_dynamic-update-slice_fusion.31
  39.7 0.9 copy.25
  40.7 1.2 fusion.22
  42.1 1.3 collective-permute-start.5
  43.4 4.2 %collective-permute-start.4 = (bf16[1,32,1,32,128]{4,1,3,2,0:T(8,128)(2,1)S(1)}, bf16[1,32,1,32,128]{4,1,3,2,0:T(8,128)(2,1)S(1)}, u32[]{:S(2)}, u32[]{:S(2)}) collective-permute-start(bf16[1,32,1,32,128]{4,1,3,2,0:T(8,128)(2,1)S(1)} %pad_maximum_fusion), channel_id=1, source_target_pairs={{0,1},{1,2},{2,3},{3,4},{4,5},{5,6},{6,7},{7,8},{8,9},{9,10},{10,1... | collective-permute-start | bytes 786440 | tf_op jit(solution)/shard_map/ppermute | solution.py:14
  47.6 1.2 fusion.37
  49.3 1.5 collective-permute-done.4
  50.7 2.3 select_maximum_fusion.3
  56.6 1.9 multiply_convert_fusion.1
  58.5 1.1 convolution_bitcast_fusion.1
  61.5 230.7 %all-reduce.7.cloned.1.call-done = f32[1,27648]{1,0:T(1,128)} async-done(((f32[1,27648]{1,0:T(1,128)}), f32[1,27648]{1,0:T(1,128)}) %all-reduce.7.cloned.1.call-update) | async-done | bytes 110608 | tf_op jit(solution)/shard_map/psum | solution.py:105
  292.2 1.7 multiply_reduce_fusion
  294.7 1.6 broadcast_multiply_fusion.1
  296.3 1.0 pad_maximum_fusion.1
  297.3 1.3 collective-permute-start.7
  298.6 4.2 %collective-permute-start.6 = (bf16[1,32,1,32,128]{4,1,3,2,0:T(8,128)(2,1)S(1)}, bf16[1,32,1,32,128]{4,1,3,2,0:T(8,128)(2,1)S(1)}, u32[]{:S(2)}, u32[]{:S(2)}) collective-permute-start(bf16[1,32,1,32,128]{4,1,3,2,0:T(8,128)(2,1)S(1)} %pad_maximum_fusion.1), channel_id=1, source_target_pairs={{0,1},{1,2},{2,3},{3,4},{4,5},{5,6},{6,7},{7,8},{8,9},{9,10},{10,1... | collective-permute-start | bytes 786440 | tf_op jit(solution)/shard_map/ppermute | solution.py:14
  302.8 25.1 %all-reduce.9.cloned.1.call-done = f32[27648]{0:T(1024)} async-done(((f32[27648]{0:T(1024)}), f32[27648]{0:T(1024)}) %all-reduce.9.cloned.1.call-update) | async-done | bytes 110608 | tf_op jit(solution)/shard_map/psum | solution.py:109
  327.9 0.9 broadcast_multiply_fusion
  329.6 3.2 select_maximum_fusion
  336.3 1.2 fusion.31
  (154 shorter events, 18.7 us)
Async XLA Ops:
  7.2 11.1 %copy-start.6 = (bf16[1,16,1,32,128]{4,3,2,1,0:T(8,128)(2,1)S(1)}, bf16[1,16,1,32,128]{4,3,2,1,0:T(8,128)(2,1)}, u32[]{:S(2)}) copy-start(bf16[1,16,1,32,128]{4,3,2,1,0:T(8,128)(2,1)} %param.6) | copy-start | bytes 393220
  7.2 285.1 %all-reduce.7.cloned.1.call-start = ((), (), s32[]{:S(2)}) async-start(), calls=%async_computation | async-start | bytes 221184 | tf_op jit(solution)/shard_map/psum | solution.py:105
  7.2 8.1 %collective-permute-start.1 = (bf16[1,16,1,32,128]{4,3,2,1,0:T(8,128)(2,1)}, bf16[1,16,1,32,128]{4,3,2,1,0:T(8,128)(2,1)S(1)}, u32[]{:S(2)}, u32[]{:S(2)}) collective-permute-start(bf16[1,16,1,32,128]{4,3,2,1,0:T(8,128)(2,1)} %param.6), channel_id=1, source_target_pairs={{1,0},{2,1},{3,2},{4,3},{5,4},{6,5},{7,6},{8,7},{9,8},{10,9},{11,1... | collective-permute-start | bytes 393224 | tf_op jit(solution)/shard_map/ppermute | solution.py:15
  8.5 6.8 %collective-permute-start = (bf16[1,16,1,32,128]{4,3,1,2,0:T(8,128)(2,1)}, bf16[1,16,1,32,128]{4,3,1,2,0:T(8,128)(2,1)S(1)}, u32[]{:S(2)}, u32[]{:S(2)}) collective-permute-start(bf16[1,16,1,32,128]{4,3,1,2,0:T(8,128)(2,1)} %bitcast.510), channel_id=1, source_target_pairs={{0,1},{1,2},{2,3},{3,4},{4,5},{5,6},{6,7},{7,8},{8,9},{9,10},{10,1... | collective-permute-start | bytes 393224 | tf_op jit(solution)/shard_map/ppermute | solution.py:14
  19.8 1.4 copy-start.11
  21.2 1.6 copy-start.7
  22.0 0.8 copy-start.4
  23.5 9.7 %collective-permute-start.3 = (bf16[1,16,1,32,128]{4,1,3,2,0:T(8,128)(2,1)}, bf16[1,16,1,32,128]{4,1,3,2,0:T(8,128)(2,1)}, u32[]{:S(2)}, u32[]{:S(2)}) collective-permute-start(bf16[1,16,1,32,128]{4,1,3,2,0:T(8,128)(2,1)} %add_convert_fusion), channel_id=1, source_target_pairs={{1,0},{2,1},{3,2},{4,3},{5,4},{6,5},{7,6},{8,7},{9,8},{10,9},{11,1... | collective-permute-start | bytes 393224 | tf_op jit(solution)/shard_map/ppermute | solution.py:15
  24.8 8.4 %collective-permute-start.2 = (bf16[1,16,1,32,128]{4,1,3,2,0:T(8,128)(2,1)}, bf16[1,16,1,32,128]{4,1,3,2,0:T(8,128)(2,1)}, u32[]{:S(2)}, u32[]{:S(2)}) collective-permute-start(bf16[1,16,1,32,128]{4,1,3,2,0:T(8,128)(2,1)} %add_convert_fusion), channel_id=1, source_target_pairs={{0,1},{1,2},{2,3},{3,4},{4,5},{5,6},{6,7},{7,8},{8,9},{9,10},{10,1... | collective-permute-start | bytes 393224 | tf_op jit(solution)/shard_map/ppermute | solution.py:14
  39.7 1.0 copy-start.12
  40.7 1.2 copy-start.9
  40.7 1.2 copy-start.13
  42.1 7.1 %collective-permute-start.5 = (bf16[1,32,1,32,128]{4,1,3,2,0:T(8,128)(2,1)S(1)}, bf16[1,32,1,32,128]{4,1,3,2,0:T(8,128)(2,1)S(1)}, u32[]{:S(2)}, u32[]{:S(2)}) collective-permute-start(bf16[1,32,1,32,128]{4,1,3,2,0:T(8,128)(2,1)S(1)} %pad_maximum_fusion), channel_id=1, source_target_pairs={{1,0},{2,1},{3,2},{4,3},{5,4},{6,5},{7,6},{8,7},{9,8},{10,9},{11,1... | collective-permute-start | bytes 786440 | tf_op jit(solution)/shard_map/ppermute | solution.py:15
  43.4 7.3 %collective-permute-start.4 = (bf16[1,32,1,32,128]{4,1,3,2,0:T(8,128)(2,1)S(1)}, bf16[1,32,1,32,128]{4,1,3,2,0:T(8,128)(2,1)S(1)}, u32[]{:S(2)}, u32[]{:S(2)}) collective-permute-start(bf16[1,32,1,32,128]{4,1,3,2,0:T(8,128)(2,1)S(1)} %pad_maximum_fusion), channel_id=1, source_target_pairs={{0,1},{1,2},{2,3},{3,4},{4,5},{5,6},{6,7},{7,8},{8,9},{9,10},{10,1... | collective-permute-start | bytes 786440 | tf_op jit(solution)/shard_map/ppermute | solution.py:14
  54.9 1.7 copy-start.5
  54.9 1.7 copy-start.10
  58.5 1.1 copy-start
  58.5 1.1 copy-start.2
  60.6 267.4 %all-reduce.9.cloned.1.call-start = ((), (), s32[]{:S(2)}) async-start(), calls=%async_computation.1 | async-start | bytes 221184 | tf_op jit(solution)/shard_map/psum | solution.py:109
  297.3 32.3 %collective-permute-start.7 = (bf16[1,32,1,32,128]{4,1,3,2,0:T(8,128)(2,1)S(1)}, bf16[1,32,1,32,128]{4,1,3,2,0:T(8,128)(2,1)S(1)}, u32[]{:S(2)}, u32[]{:S(2)}) collective-permute-start(bf16[1,32,1,32,128]{4,1,3,2,0:T(8,128)(2,1)S(1)} %pad_maximum_fusion.1), channel_id=1, source_target_pairs={{1,0},{2,1},{3,2},{4,3},{5,4},{6,5},{7,6},{8,7},{9,8},{10,9},{11,1... | collective-permute-start | bytes 786440 | tf_op jit(solution)/shard_map/ppermute | solution.py:15
  298.6 31.1 %collective-permute-start.6 = (bf16[1,32,1,32,128]{4,1,3,2,0:T(8,128)(2,1)S(1)}, bf16[1,32,1,32,128]{4,1,3,2,0:T(8,128)(2,1)S(1)}, u32[]{:S(2)}, u32[]{:S(2)}) collective-permute-start(bf16[1,32,1,32,128]{4,1,3,2,0:T(8,128)(2,1)S(1)} %pad_maximum_fusion.1), channel_id=1, source_target_pairs={{0,1},{1,2},{2,3},{3,4},{4,5},{5,6},{6,7},{7,8},{8,9},{9,10},{10,1... | collective-permute-start | bytes 786440 | tf_op jit(solution)/shard_map/ppermute | solution.py:14
  332.8 1.8 copy-start.1
  332.8 1.8 copy-start.3
  334.6 1.7 copy-start.8
Sparse Core Ops, SparseCore 0:
  60.7 231.5 all-reduce.6
  296.4 31.4 all-reduce.8
where the time goes:
time: 346 us; the launch traced here: 345 us
  waiting for transfers between devices  259 us (75%)
  starting transfers between devices  23.2 us (7%)
  local copies, waits for them, and re-layouts  22.9 us (7%)
  between operations  16.9 us (5%)
  other arithmetic  16.1 us (5%)
  matrix products  7.43 us (2%)
    psum x1, waiting for transfers between devices, per_device(): summed = lax.psum(flat, 'slab')  231 us
    psum x1, waiting for transfers between devices, per_device(): total = lax.psum(local_total, 'ex')  25.1 us
    ppermute x4, starting transfers between devices, with_halo(): before = lax.ppermute(last, axis, up)  17.9 us
    unnamed x131, local copies, waits for them, and re-layouts  15.5 us
    concatenate x4, other arithmetic, with_halo(): array = jnp.concatenate([before, array, after], axis=dim)  8.49 us
  transfers between devices with their start and end apart: 10, of which 5 were waited for; matrix products, arithmetic and copies ran while one was open for 2% of the time, Pallas kernels for 0%

commit v1 on v0

v1 whole, which is shorter than its diff:
```python
import functools
import jax
import jax.numpy as jnp
from jax import lax
from jax.experimental import pallas as pl
from jax.experimental.pallas import tpu as pltpu
from jax.sharding import PartitionSpec as P

F32 = jnp.float32
BF16 = jnp.bfloat16
MESH = pl.DeviceIdType.MESH
C = 16
H = 32
W = 128
NC = 4
HC = H // NC
CW = HC * W
PW = (H + 2) * W


def torus_of(slabs):
    return {128: (4, 4, 8), 8: (2, 2, 2)}[slabs]


def kernel(torus, depth, vol, cot, mask, scale, canary, ker, dx_out, kg_out,
           tmp, xb, db, kbt, kb, mk, a1, b1, dy, own, bsend, brecv, gpad,
           gs, rsr, zr, ag, ps, pr,
           xs_sem, xr_sem, bs_sem, br_sem, rs_s, rs_r, z_s, z_r, ag_s, ag_r, p_s, p_r):
    nx, ny, nz = torus
    gxy = nx * ny
    slabs = gxy * nz
    me = lax.axis_index("slab")
    ex = lax.axis_index("ex")
    up = lax.rem(me + 1, slabs)
    down = lax.rem(me + slabs - 1, slabs)
    mz = me // gxy
    mxy = lax.rem(me, gxy)
    my = mxy // nx
    mx = lax.rem(mxy, nx)
    offs = [(a, b) for b in range(ny) for a in range(nx) if (a, b) != (0, 0)]
    offs.sort(key=lambda o: -(min(o[0], nx - o[0]) + min(o[1], ny - o[1])))
    zoffs = sorted(range(1, nz), key=lambda o: -min(o, nz - o))

    def xy_peer(o):
        return lax.rem(my + o[1], ny) * nx + lax.rem(mx + o[0], nx)

    barrier = pltpu.get_barrier_semaphore()
    for t in (up, down):
        pl.semaphore_signal(barrier, inc=1, device_id={"slab": t}, device_id_type=MESH)
    for o in offs:
        pl.semaphore_signal(barrier, inc=1, device_id={"slab": mz * gxy + xy_peer(o)}, device_id_type=MESH)
    for o in zoffs:
        pl.semaphore_signal(barrier, inc=1, device_id={"slab": lax.rem(mz + o, nz) * gxy + mxy}, device_id_type=MESH)
    pl.semaphore_signal(barrier, inc=1, device_id={"ex": 1 - ex}, device_id_type=MESH)

    lane = lax.broadcasted_iota(jnp.int32, (C, W), 1)
    first = lane == 0
    last = lane == W - 1
    has_down = me > 0
    has_up = me < slabs - 1

    def shifts(x):
        rows = x.shape[0] // C
        left, right = [], []
        for i in range(rows):
            part = x[i * C:(i + 1) * C, :].astype(F32)
            left.append(jnp.where(first, 0.0, pltpu.roll(part, 1, 1)).astype(BF16))
            right.append(jnp.where(last, 0.0, pltpu.roll(part, W - 1, 1)).astype(BF16))
        if rows == 1:
            return left[0], right[0]
        return jnp.concatenate(left, axis=0), jnp.concatenate(right, axis=0)

    def fill(layer, dz, k):
        for i in range(HC):
            at = pl.ds((1 + k * HC + i) * W, W)
            x = xb[layer, dz * 3 + 1, :, at]
            if dz != 1:
                x = jnp.where(has_down if dz == 0 else has_up, x.astype(F32), 0.0).astype(BF16)
                xb[layer, dz * 3 + 1, :, at] = x
            left, right = shifts(x)
            xb[layer, dz * 3, :, at] = left
            xb[layer, dz * 3 + 2, :, at] = right

    def cols(layer, k):
        parts = []
        for dz in range(3):
            for dh in range(3):
                for dw in range(3):
                    parts.append(xb[layer, dz * 3 + dw, :, pl.ds((k * HC + dh) * W, CW)])
        return jnp.concatenate(parts, axis=0)

    def back_cols(layer, k):
        parts = []
        for dh in range(3):
            for dw in range(3):
                parts.append(db[layer, dw, :, pl.ds((k * HC + 2 - dh) * W, CW)])
        return jnp.concatenate(parts, axis=0)

    def halo_copies(layer, k):
        at = pl.ds((1 + k * HC) * W, CW)
        src = xb.at[layer, 4, :, at]
        made = []
        for side, (dz, peer) in enumerate(((0, up), (2, down))):
            made.append(pltpu.make_async_remote_copy(
                src_ref=src, dst_ref=xb.at[layer, dz * 3 + 1, :, at],
                send_sem=xs_sem.at[layer, side, k], recv_sem=xr_sem.at[layer, side, k],
                device_id={"slab": peer}, device_id_type=MESH))
        return made

    def back_copies(layer, k):
        at = pl.ds(k * CW, CW)
        made = []
        for side, peer in enumerate((up, down)):
            made.append(pltpu.make_async_remote_copy(
                src_ref=bsend.at[layer, side, :, at], dst_ref=brecv.at[layer, side, :, at],
                send_sem=bs_sem.at[layer, side, k], recv_sem=br_sem.at[layer, side, k],
                device_id={"slab": peer}, device_id_type=MESH))
        return made

    def store_delta(layer, k, delta):
        for i in range(HC):
            at = pl.ds((1 + k * HC + i) * W, W)
            x = delta[:, i * W:(i + 1) * W]
            left, right = shifts(x)
            db[layer, 1, :, at] = x
            db[layer, 2, :, at] = left
            db[layer, 0, :, at] = right

    def back(layer, k):
        got = jnp.dot(kb[layer], back_cols(layer, k), preferred_element_type=F32)
        at = pl.ds(k * CW, CW)
        own[:, at] = got[C:2 * C]
        bsend[layer, 1, :, at] = got[:C].astype(BF16)
        bsend[layer, 0, :, at] = got[2 * C:].astype(BF16)

    def back_total(layer, k):
        at = pl.ds(k * CW, CW)
        below = jnp.where(has_down, brecv[layer, 0, :, at].astype(F32), 0.0)
        above = jnp.where(has_up, brecv[layer, 1, :, at].astype(F32), 0.0)
        return own[:, at] + below + above

    def weight_grad(layer, k):
        d = db[layer, 1, :, pl.ds((1 + k * HC) * W, CW)]
        return lax.dot_general(d, cols(layer, k), (((1,), (1,)), ((), ())), preferred_element_type=F32)

    tmp[...] = vol[...].astype(F32)
    for h in range(H):
        xb[0, 4, :, pl.ds((1 + h) * W, W)] = tmp[:, h, :].astype(BF16)
    zero_row = jnp.zeros((C, W), BF16)
    for edge in (0, H + 1):
        at = pl.ds(edge * W, W)
        for layer in range(2):
            for q in range(9):
                xb[layer, q, :, at] = zero_row
            for q in range(3):
                db[layer, q, :C, at] = zero_row
                db[layer, q, C:, at] = zero_row
    gpad[...] = jnp.zeros_like(gpad)
    pl.semaphore_wait(barrier, 2 + len(offs) + len(zoffs) + 1)

    for k in range(NC):
        for copy in halo_copies(0, k):
            copy.start()

    for k in range(NC):
        fill(0, 1, k)
    for h in range(H):
        for q in range(2):
            row = mask[q, h:h + 1, :].astype(F32)
            mk[q, :, pl.ds(h * W, W)] = jnp.broadcast_to(row, (C, W))
    for layer in range(2):
        kf = ker[layer].astype(F32)
        for dh in range(3):
            for dw in range(3):
                for dz in range(3):
                    t = 9 * dz + 3 * dh + dw
                    kbt[pl.ds((dh * 3 + dw) * 2 * C, 2 * C), dz * C:(dz + 1) * C] = kf[:, t * C:(t + 1) * C]
        kb[layer] = jnp.transpose(kbt[...])[:3 * C].astype(BF16)
    tmp[...] = cot[...].astype(F32)
    chan = lax.broadcasted_iota(jnp.int32, (C, W), 0)
    weight = jnp.where(chan == canary[0], 3.0, 1.0).astype(F32)
    for h in range(H):
        dy[:, pl.ds(h * W, W)] = tmp[:, h, :] * scale[0] * weight

    def layer_one(k):
        pre = jnp.dot(ker[0], cols(0, k), preferred_element_type=F32)
        at = pl.ds(k * CW, CW)
        pat = pl.ds((1 + k * HC) * W, CW)
        v = pre[:C]
        s = jax.nn.sigmoid(pre[C:])
        sm = s * mk[0, :, at]
        a1[:, at] = sm
        b1[:, at] = v * sm * (1.0 - s)
        xb[1, 4, :, pat] = (xb[0, 4, :, pat].astype(F32) + v * sm).astype(BF16)
        for copy in halo_copies(1, k):
            copy.start()
        fill(1, 1, k)

    for k in range(NC):
        for copy in halo_copies(0, k):
            copy.wait_recv()
        fill(0, 0, k)
        fill(0, 2, k)
        if k > 0:
            layer_one(k - 1)
    layer_one(NC - 1)

    def layer_two(k):
        pre = jnp.dot(ker[1], cols(1, k), preferred_element_type=F32)
        at = pl.ds(k * CW, CW)
        v = pre[:C]
        s = jax.nn.sigmoid(pre[C:])
        g = dy[:, at] * (s * mk[1, :, at])
        delta = jnp.concatenate([g, g * v * (1.0 - s)], axis=0).astype(BF16)
        store_delta(1, k, delta)

    def back_send(layer, k):
        back(layer, k)
        for copy in back_copies(layer, k):
            copy.start()

    for k in range(NC):
        for copy in halo_copies(1, k):
            copy.wait_recv()
        fill(1, 0, k)
        fill(1, 2, k)
        if k > 0:
            layer_two(k - 1)
        if k > 1:
            back_send(1, k - 2)
    layer_two(NC - 1)
    back_send(1, NC - 2)
    back_send(1, NC - 1)

    g2 = weight_grad(1, 0)
    for k in range(1, NC):
        g2 = g2 + weight_grad(1, k)
    gpad[1, :, :27 * C] = g2

    g1 = None
    for k in range(NC):
        at = pl.ds(k * CW, CW)
        for copy in back_copies(1, k):
            copy.wait_recv()
        dx = dy[:, at] + back_total(1, k)
        dy[:, at] = dx
        delta = jnp.concatenate([dx * a1[:, at], dx * b1[:, at]], axis=0).astype(BF16)
        store_delta(0, k, delta)
        part = weight_grad(0, k)
        g1 = part if k == 0 else g1 + part
    gpad[0, :, :27 * C] = g1

    tiles = 16 // gxy
    for j in range(16):
        i, n = j // 4, j % 4
        for layer in range(2):
            gs[j // tiles, layer, j % tiles] = gpad[layer, i * 8:(i + 1) * 8, n * W:(n + 1) * W]

    def rs_copy(o):
        r = o[1] * nx + o[0]
        peer = xy_peer(o)
        return pltpu.make_async_remote_copy(
            src_ref=gs.at[peer], dst_ref=rsr.at[r], send_sem=rs_s.at[r], recv_sem=rs_r.at[r],
            device_id={"slab": mz * gxy + peer}, device_id_type=MESH)

    def z_copy(o):
        return pltpu.make_async_remote_copy(
            src_ref=zr.at[mz], dst_ref=zr.at[mz], send_sem=z_s.at[o], recv_sem=z_r.at[o],
            device_id={"slab": lax.rem(mz + o, nz) * gxy + mxy}, device_id_type=MESH)

    def ag_copy(o):
        r = o[1] * nx + o[0]
        return pltpu.make_async_remote_copy(
            src_ref=ag.at[mxy], dst_ref=ag.at[mxy], send_sem=ag_s.at[r], recv_sem=ag_r.at[r],
            device_id={"slab": mz * gxy + xy_peer(o)}, device_id_type=MESH)

    for o in offs:
        rs_copy(o).start()
    for k in range(NC):
        back_send(0, k)
    for o in offs:
        rs_copy(o).wait_recv()
    total = gs[mxy]
    for o in offs:
        total = total + rsr[o[1] * nx + o[0]]
    zr[mz] = total
    for o in zoffs:
        z_copy(o).start()

    for k in range(NC):
        for copy in back_copies(0, k):
            copy.wait_recv()
        at = pl.ds(k * CW, CW)
        res = dy[:, at] + back_total(0, k)
        for i in range(HC):
            dx_out[:, k * HC + i, :] = res[:, i * W:(i + 1) * W]

    for o in zoffs:
        z_copy(o).wait()
    total = zr[0]
    for q in range(1, nz):
        total = total + zr[q]
    ag[mxy] = total
    for o in offs:
        ag_copy(o).start()
    for o in offs:
        ag_copy(o).wait()

    bound = 20.0 * float(depth * H * W) ** 0.5
    square = None
    for q in range(gxy):
        for layer in range(2):
            for t in range(tiles):
                x = ag[q, layer, t]
                square = x * x if square is None else square + x * x
    norm = jnp.sqrt(jnp.sum(square, keepdims=True) + 1e-06)
    scaling = float(108 * C * C) ** 0.5 / (bound * 2.0 ** 0.5)
    factor = jnp.minimum(1.0, bound / norm)
    for q in range(gxy):
        for layer in range(2):
            for t in range(tiles):
                ps[q, layer, t] = ag[q, layer, t] * factor
    swap = pltpu.make_async_remote_copy(
        src_ref=ps, dst_ref=pr, send_sem=p_s, recv_sem=p_r,
        device_id={"ex": 1 - ex}, device_id_type=MESH)
    swap.start()
    swap.wait()
    for j in range(16):
        i, n = j // 4, j % 4
        width = min(W, 27 * C - n * W)
        for layer in range(2):
            x = (ps[j // tiles, layer, j % tiles] + pr[j // tiles, layer, j % tiles]) * scaling
            kg_out[layer, i * 8:(i + 1) * 8, n * W:n * W + width] = x[:, :width]

    for k in range(NC):
        for layer in range(2):
            for copy in halo_copies(layer, k):
                copy.wait_send()
            for copy in back_copies(layer, k):
                copy.wait_send()
    for o in offs:
        rs_copy(o).wait_send()


def per_device(volume, cotangent, gate_mask, loss_scale, canary, kernels):
    slabs = lax.axis_size("slab")
    torus = torus_of(slabs)
    nx, ny, nz = torus
    gxy = nx * ny
    tiles = 16 // gxy
    vm = pl.BlockSpec(memory_space=pltpu.VMEM)
    sm = pl.BlockSpec(memory_space=pltpu.SMEM)
    dma = pltpu.SemaphoreType.DMA
    part = (2, tiles, 8, W)
    dx, kg = pl.pallas_call(
        functools.partial(kernel, torus, slabs),
        out_shape=(jax.ShapeDtypeStruct((C, H, W), F32), jax.ShapeDtypeStruct((2, 2 * C, 27 * C), F32)),
        in_specs=[vm, vm, vm, sm, sm, vm],
        out_specs=(vm, vm),
        scratch_shapes=[
            pltpu.VMEM((C, H, W), F32),
            pltpu.VMEM((2, 9, C, PW), BF16),
            pltpu.VMEM((2, 3, 2 * C, PW), BF16),
            pltpu.VMEM((18 * C, W), F32),
            pltpu.VMEM((2, 3 * C, 18 * C), BF16),
            pltpu.VMEM((2, C, H * W), F32),
            pltpu.VMEM((C, H * W), F32),
            pltpu.VMEM((C, H * W), F32),
            pltpu.VMEM((C, H * W), F32),
            pltpu.VMEM((C, H * W), F32),
            pltpu.VMEM((2, 2, C, H * W), BF16),
            pltpu.VMEM((2, 2, C, H * W), BF16),
            pltpu.VMEM((2, 2 * C, 4 * W), F32),
            pltpu.VMEM((gxy,) + part, F32),
            pltpu.VMEM((gxy,) + part, F32),
            pltpu.VMEM((nz,) + part, F32),
            pltpu.VMEM((gxy,) + part, F32),
            pltpu.VMEM((gxy,) + part, F32),
            pltpu.VMEM((gxy,) + part, F32),
            dma((2, 2, NC)), dma((2, 2, NC)), dma((2, 2, NC)), dma((2, 2, NC)),
            dma((gxy,)), dma((gxy,)), dma((nz,)), dma((nz,)), dma((gxy,)), dma((gxy,)),
            dma, dma,
        ],
        compiler_params=pltpu.CompilerParams(
            collective_id=0, has_side_effects=True, vmem_limit_bytes=48 * 1024 * 1024),
        name="gated_level",
    )(
        volume.reshape((C, H, W)),
        cotangent.reshape((C, H, W)),
        gate_mask.reshape((2, H, W)),
        loss_scale,
        canary,
        kernels,
    )
    return dx.reshape((1, C, 1, H, W)), kg


def solution(mesh):
    placed = (
        P("ex", None, "slab", None, None),
        P("ex", None, "slab", None, None),
        P("ex", None, "slab", None, None),
        P("ex"),
        P("ex"),
        P(),
    )
    return jax.shard_map(
        per_device,
        mesh=mesh,
        in_specs=placed,
        out_specs=(P("ex", None, "slab", None, None), P()),
        check_vma=False,
    )
```

time: 346 us -> 56 us (0.16)
  waiting for transfers between devices: 259 us -> 0 us
  Pallas kernels: 0 us -> 49 us
  starting transfers between devices: 23.2 us -> 0 us
  local copies, waits for them, and re-layouts: 22.9 us -> 4.76 us
  other arithmetic: 16.1 us -> 0 us
  between operations: 16.9 us -> 1.94 us
  matrix products: 7.43 us -> 0 us
    psum x2 -> x0, waiting for transfers between devices: 256 us -> none  [the longest x1 231 us: per_device(): summed = lax.psum(flat, 'slab')]
    pallas_call x0 -> x1, Pallas kernels: none -> 49 us  [per_device(): pl.pallas_call(functools.partial(kernel, torus, slabs), out_shape=(jax.Sh...]
    ppermute x8 -> x0, starting transfers between devices: 23.1 us -> none  [the longest x4 17.9 us: with_halo(): before = lax.ppermute(last, axis, up)]
    unnamed x131 -> x10, local copies, waits for them, and re-layouts: 15.5 us -> 4.76 us
    concatenate x6 -> x0, other arithmetic: 9.5 us -> none  [the longest x4 8.49 us: with_halo(): array = jnp.concatenate([before, array, after], axis=dim)]
    dot_general x6 -> x0, matrix products: 7.43 us -> none  [the longest x2 3.18 us: layer_backward(): jnp.einsum('otc,etozhw->eczhw', shaped, back_columns(extended), preferred...]
    mul x4 -> x0, other arithmetic: 3.87 us -> none  [the longest x1 1.62 us: per_device(): local_total = jnp.sum(summed * factor[:, None], axis=0)]
  transfers between devices with their start and end apart: 10 -> 0, of which waited for: 5 -> 0; matrix products, arithmetic and copies ran while one was open for 2% -> 0% of each run, Pallas kernels for 0% -> 0%
where the time goes in v1:
time: 56 us; the launch traced here: 55.7 us
  Pallas kernels  49 us (88%)
  local copies, waits for them, and re-layouts  4.76 us (8%)
  between operations  1.94 us (3%)
    pallas_call x1, Pallas kernels, per_device(): pl.pallas_call(functools.partial(kernel, torus, slabs), out_shape=(jax.Sh...  49 us
    unnamed x10, local copies, waits for them, and re-layouts  4.76 us

profile of v1, /device:TPU:1, one launch (start us, length us, event | category | flops | bytes accessed | tf_op | source)
XLA Modules:
  0.0 55.7 jit_solution(1203357266823306872)
XLA Ops:
  1.9 0.0 copy-start
  1.9 0.9 %copy-done = bf16[1,16,1,32,128]{4,3,2,1,0:T(8,128)(2,1)S(1)} copy-done((bf16[1,16,1,32,128]{4,3,2,1,0:T(8,128)(2,1)S(1)}, bf16[1,16,1,32,128]{4,3,2,1,0:T(8,128)(2,1)}, u32[]{:S(2)}) %copy-start) | copy-done | bytes 131096
  2.8 0.0 copy-start.1
  2.8 0.9 %copy-done.1 = bf16[1,16,1,32,128]{4,3,2,1,0:T(8,128)(2,1)S(1)} copy-done((bf16[1,16,1,32,128]{4,3,2,1,0:T(8,128)(2,1)S(1)}, bf16[1,16,1,32,128]{4,3,2,1,0:T(8,128)(2,1)}, u32[]{:S(2)}) %copy-start.1) | copy-done | bytes 131096
  3.7 0.0 copy-start.2
  3.7 0.8 %copy-done.2 = bf16[2,32,432]{2,1,0:T(8,128)(2,1)S(1)} copy-done((bf16[2,32,432]{2,1,0:T(8,128)(2,1)S(1)}, bf16[2,32,432]{2,1,0:T(8,128)(2,1)}, u32[]{:S(2)}) %copy-start.2) | copy-done | bytes 55320
  4.6 0.0 copy-start.3
  4.6 0.8 %copy-done.3 = s32[1,2,1,32,128]{4,3,2,1,0:T(8,128)S(1)} copy-done((s32[1,2,1,32,128]{4,3,2,1,0:T(8,128)S(1)}, s32[1,2,1,32,128]{4,3,2,1,0:T(8,128)}, u32[]{:S(2)}) %copy-start.3) | copy-done | bytes 32792
  5.3 49.0 %gated_level.1 = (f32[16,32,128]{2,1,0:T(8,128)S(1)}, f32[2,32,432]{2,1,0:T(8,128)S(1)}) custom-call(bf16[16,32,128]{2,1,0:T(8,128)(2,1)S(1)} %bitcast.7, bf16[16,32,128]{2,1,0:T(8,128)(2,1)S(1)} %bitcast.8, s32[2,32,128]{2,1,0:T(8,128)S(1)} %bitcast.9, f32[1]{0:T(128)S(6)} %copy.11.scale, s32[1]{0:T(128)S(6)} %copy.12.canary, bf16[2,32,432]{2,1,0:T(8,128)(2,1)S(1)} %copy-done.2), custom_call_target="tpu_custom_call" | custom-call | tf_op jit(solution)/shard_map/gated_level/pallas_call | solution.py:355
  54.4 0.7 %copy.13 = f32[1,16,1,32,128]{4,3,2,1,0:T(8,128)} copy(f32[1,16,1,32,128]{4,3,2,1,0:T(8,128)S(1)} %bitcast.6) | data formatting | bytes 524288
  55.1 0.7 %copy.14 = f32[2,32,432]{2,1,0:T(8,128)} copy(f32[2,32,432]{2,1,0:T(8,128)S(1)} %get-tuple-element.11) | data formatting | bytes 221184
Async XLA Ops:
  1.9 0.9 %copy-start = (bf16[1,16,1,32,128]{4,3,2,1,0:T(8,128)(2,1)S(1)}, bf16[1,16,1,32,128]{4,3,2,1,0:T(8,128)(2,1)}, u32[]{:S(2)}) copy-start(bf16[1,16,1,32,128]{4,3,2,1,0:T(8,128)(2,1)} %param.6) | copy-start | bytes 393220
  2.8 0.9 %copy-start.1 = (bf16[1,16,1,32,128]{4,3,2,1,0:T(8,128)(2,1)S(1)}, bf16[1,16,1,32,128]{4,3,2,1,0:T(8,128)(2,1)}, u32[]{:S(2)}) copy-start(bf16[1,16,1,32,128]{4,3,2,1,0:T(8,128)(2,1)} %param.7) | copy-start | bytes 393220
  3.7 0.8 %copy-start.2 = (bf16[2,32,432]{2,1,0:T(8,128)(2,1)S(1)}, bf16[2,32,432]{2,1,0:T(8,128)(2,1)}, u32[]{:S(2)}) copy-start(bf16[2,32,432]{2,1,0:T(8,128)(2,1)} %ker.1) | copy-start | bytes 165892
  4.6 0.8 %copy-start.3 = (s32[1,2,1,32,128]{4,3,2,1,0:T(8,128)S(1)}, s32[1,2,1,32,128]{4,3,2,1,0:T(8,128)}, u32[]{:S(2)}) copy-start(s32[1,2,1,32,128]{4,3,2,1,0:T(8,128)} %param.8) | copy-start | bytes 98308

commit v2 on v1

v2 whole, which is shorter than its diff:
```python
import functools
import jax
import jax.numpy as jnp
from jax import lax
from jax.experimental import pallas as pl
from jax.experimental.pallas import tpu as pltpu
from jax.sharding import PartitionSpec as P

F32 = jnp.float32
BF16 = jnp.bfloat16
MESH = pl.DeviceIdType.MESH
C = 16
H = 32
W = 128
PW = (H + 2) * W
ROWS = (
    (0, 10, 20, 28, 32),
    (0, 9, 19, 27, 32),
    (0, 8, 18, 26, 32),
    (0, 7, 17, 25, 32),
)
NC = len(ROWS[0]) - 1


def torus_of(slabs):
    return {128: (4, 4, 8), 8: (2, 2, 2)}[slabs]


def spans(stage, k):
    return ROWS[stage][k], ROWS[stage][k + 1]


def flat(r0, r1):
    return pl.ds(r0 * W, (r1 - r0) * W)


def kernel(torus, depth, vol_hbm, cot_hbm, mask_hbm, scale, canary, ker_hbm, dx_out, kg_out,
           vol, cot, mask, ker, tmp, xb, db, kbt, kb, mk, a1, b1, dy, own, bsend, brecv, gpad,
           gs, rsr, zr, ag, kgs,
           xs_sem, xr_sem, bs_sem, br_sem, rs_s, rs_r, z_s, z_r, ag_s, ag_r, p_s, p_r, in_sem):
    nx, ny, nz = torus
    gxy = nx * ny
    slabs = gxy * nz
    me = lax.axis_index("slab")
    ex = lax.axis_index("ex")
    mz = me // gxy
    mxy = lax.rem(me, gxy)
    my = mxy // nx
    mx = lax.rem(mxy, nx)
    offs = [(a, b) for b in range(ny) for a in range(nx) if (a, b) != (0, 0)]
    offs.sort(key=lambda o: -(min(o[0], nx - o[0]) + min(o[1], ny - o[1])))
    zoffs = sorted(range(1, nz), key=lambda o: -min(o, nz - o))
    tiles = 16 // gxy
    slots = ((1, 1), (1, 0), (0, 1), (0, 0))
    groups = ((0, 3), (3, 1))
    has_down = me > 0
    has_up = me < slabs - 1
    up = jnp.minimum(me + 1, slabs - 1)
    down = jnp.maximum(me - 1, 0)

    def xy_peer(o):
        return lax.rem(my + o[1], ny) * nx + lax.rem(mx + o[0], nx)

    def signal(device):
        pl.semaphore_signal(barrier, inc=1, device_id=device, device_id_type=MESH)

    barrier = pltpu.get_barrier_semaphore()

    @pl.when(has_up)
    def _():
        signal({"slab": up})

    @pl.when(has_down)
    def _():
        signal({"slab": down})

    @pl.when(ex == 1)
    def _():
        for o in offs:
            for e in range(2):
                signal({"ex": e, "slab": mz * gxy + xy_peer(o)})
        for o in zoffs:
            signal({"slab": lax.rem(mz + o, nz) * gxy + mxy})

    signal({"ex": 1 - ex})
    loads = [pltpu.make_async_copy(src, dst, in_sem.at[q]) for q, (src, dst) in enumerate(
        ((vol_hbm, vol), (ker_hbm, ker), (mask_hbm, mask), (cot_hbm, cot)))]
    for load in loads:
        load.start()
    lane = lax.broadcasted_iota(jnp.int32, (C, W), 1)
    first = lane == 0
    last = lane == W - 1

    def shifts(x):
        rows = x.shape[0] // C
        left, right = [], []
        for i in range(rows):
            part = x[i * C:(i + 1) * C, :].astype(F32)
            left.append(jnp.where(first, 0.0, pltpu.roll(part, 1, 1)).astype(BF16))
            right.append(jnp.where(last, 0.0, pltpu.roll(part, W - 1, 1)).astype(BF16))
        if rows == 1:
            return left[0], right[0]
        return jnp.concatenate(left, axis=0), jnp.concatenate(right, axis=0)

    def fill(layer, dz, rows):
        for r in range(*rows):
            at = flat(1 + r, 2 + r)
            x = xb[layer, dz * 3 + 1, :, at]
            if dz != 1:
                x = jnp.where(has_down if dz == 0 else has_up, x.astype(F32), 0.0).astype(BF16)
                xb[layer, dz * 3 + 1, :, at] = x
            left, right = shifts(x)
            xb[layer, dz * 3, :, at] = left
            xb[layer, dz * 3 + 2, :, at] = right

    def cols(layer, rows):
        parts = []
        for dz in range(3):
            for dh in range(3):
                for dw in range(3):
                    parts.append(xb[layer, dz * 3 + dw, :, flat(rows[0] + dh, rows[1] + dh)])
        return jnp.concatenate(parts, axis=0)

    def back_cols(layer, rows):
        parts = []
        for dh in range(3):
            for dw in range(3):
                parts.append(db[layer, dw, :, flat(rows[0] + 2 - dh, rows[1] + 2 - dh)])
        return jnp.concatenate(parts, axis=0)

    def halo_copy(layer, side, k):
        r0, r1 = spans(layer, k)
        at = flat(1 + r0, 1 + r1)
        return pltpu.make_async_remote_copy(
            src_ref=xb.at[layer, 4, :, at], dst_ref=xb.at[layer, 6 * side + 1, :, at],
            send_sem=xs_sem.at[layer, side, k], recv_sem=xr_sem.at[layer, side, k],
            device_id={"slab": (up, down)[side]}, device_id_type=MESH)

    def back_copy(layer, side, k):
        at = flat(*spans(3, k))
        return pltpu.make_async_remote_copy(
            src_ref=bsend.at[layer, side, :, at], dst_ref=brecv.at[layer, side, :, at],
            send_sem=bs_sem.at[layer, side, k], recv_sem=br_sem.at[layer, side, k],
            device_id={"slab": (up, down)[side]}, device_id_type=MESH)

    def start(copy, layer, k):
        @pl.when(has_up)
        def _():
            copy(layer, 0, k).start()

        @pl.when(has_down)
        def _():
            copy(layer, 1, k).start()

    def arrive(copy, layer, k):
        @pl.when(has_down)
        def _():
            copy(layer, 0, k).wait_recv()

        @pl.when(has_up)
        def _():
            copy(layer, 1, k).wait_recv()

    def sent(copy, layer):
        @pl.when(has_up)
        def _():
            for k in range(NC):
                copy(layer, 0, k).wait_send()

        @pl.when(has_down)
        def _():
            for k in range(NC):
                copy(layer, 1, k).wait_send()

    def store_delta(layer, rows, delta):
        for i, r in enumerate(range(*rows)):
            at = flat(1 + r, 2 + r)
            x = delta[:, i * W:(i + 1) * W]
            left, right = shifts(x)
            db[layer, 1, :, at] = x
            db[layer, 2, :, at] = left
            db[layer, 0, :, at] = right

    def back(layer, rows):
        got = jnp.dot(kb[layer], back_cols(layer, rows), preferred_element_type=F32)
        at = flat(*rows)
        own[:, at] = got[C:2 * C]
        bsend[layer, 1, :, at] = got[:C].astype(BF16)
        bsend[layer, 0, :, at] = got[2 * C:].astype(BF16)

    def back_total(layer, rows):
        at = flat(*rows)
        below = jnp.where(has_down, brecv[layer, 0, :, at].astype(F32), 0.0)
        above = jnp.where(has_up, brecv[layer, 1, :, at].astype(F32), 0.0)
        return own[:, at] + below + above

    def weight_grad(layer, rows):
        d = db[layer, 1, :, flat(1 + rows[0], 1 + rows[1])]
        return lax.dot_general(d, cols(layer, rows), (((1,), (1,)), ((), ())), preferred_element_type=F32)

    loads[0].wait()
    tmp[...] = vol[...].astype(F32)
    for h in range(H):
        xb[0, 4, :, flat(1 + h, 2 + h)] = tmp[:, h, :].astype(BF16)
    zero_row = jnp.zeros((C, W), BF16)
    for edge in (0, H + 1):
        at = flat(edge, edge + 1)
        for layer in range(2):
            for q in range(9):
                xb[layer, q, :, at] = zero_row
            for q in range(3):
                db[layer, q, :C, at] = zero_row
                db[layer, q, C:, at] = zero_row
    gpad[...] = jnp.zeros_like(gpad)
    many = jnp.where(ex == 1, len(offs) + len(zoffs) + 1, len(offs) + 1)
    pl.semaphore_wait(barrier, many + has_up.astype(jnp.int32) + has_down.astype(jnp.int32))
    for k in range(NC):
        start(halo_copy, 0, k)
    fill(0, 1, (0, H))
    for load in loads[1:]:
        load.wait()
    for h in range(H):
        for q in range(2):
            row = mask[q, h:h + 1, :].astype(F32)
            mk[q, :, flat(h, h + 1)] = jnp.broadcast_to(row, (C, W))
    for layer in range(2):
        kf = ker[layer].astype(F32)
        for dh in range(3):
            for dw in range(3):
                for dz in range(3):
                    t = 9 * dz + 3 * dh + dw
                    kbt[pl.ds((dh * 3 + dw) * 2 * C, 2 * C), dz * C:(dz + 1) * C] = kf[:, t * C:(t + 1) * C]
        kb[layer] = jnp.transpose(kbt[...])[:3 * C].astype(BF16)
    tmp[...] = cot[...].astype(F32)
    chan = lax.broadcasted_iota(jnp.int32, (C, W), 0)
    weight = jnp.where(chan == canary[0], 3.0, 1.0).astype(F32)
    for h in range(H):
        dy[:, flat(h, h + 1)] = tmp[:, h, :] * scale[0] * weight

    def layer_one(rows):
        pre = jnp.dot(ker[0], cols(0, rows), preferred_element_type=F32)
        at = flat(*rows)
        pat = flat(1 + rows[0], 1 + rows[1])
        v = pre[:C]
        s = jax.nn.sigmoid(pre[C:])
        sm = s * mk[0, :, at]
        a1[:, at] = sm
        b1[:, at] = v * sm * (1.0 - s)
        xb[1, 4, :, pat] = (xb[0, 4, :, pat].astype(F32) + v * sm).astype(BF16)

    def layer_two(rows):
        pre = jnp.dot(ker[1], cols(1, rows), preferred_element_type=F32)
        at = flat(*rows)
        v = pre[:C]
        s = jax.nn.sigmoid(pre[C:])
        g = dy[:, at] * (s * mk[1, :, at])
        delta = jnp.concatenate([g, g * v * (1.0 - s)], axis=0).astype(BF16)
        store_delta(1, rows, delta)

    def spread(layer, g):
        gpad[layer, :, :27 * C] = g
        for j in range(16):
            i, n = j // 4, j % 4
            gs[layer, j // tiles, j % tiles] = gpad[layer, i * 8:(i + 1) * 8, n * W:(n + 1) * W]

    def rs_copy(layer, o, e):
        r = o[1] * nx + o[0]
        peer = xy_peer(o)
        return pltpu.make_async_remote_copy(
            src_ref=gs.at[layer, peer], dst_ref=rsr.at[e, layer, r],
            send_sem=rs_s.at[layer, r], recv_sem=rs_r.at[e, layer, r],
            device_id={"ex": 1, "slab": mz * gxy + peer}, device_id_type=MESH)

    def rs_start(layer):
        for o in offs:
            rs_copy(layer, o, ex).start()

        @pl.when(ex == 0)
        def _():
            rs_copy(layer, (0, 0), 0).start()

    def z_copy(group, o):
        at = pl.ds(*groups[group])
        return pltpu.make_async_remote_copy(
            src_ref=zr.at[mz, at], dst_ref=zr.at[mz, at],
            send_sem=z_s.at[group, o], recv_sem=z_r.at[group, o],
            device_id={"slab": lax.rem(mz + o, nz) * gxy + mxy}, device_id_type=MESH)

    def ag_copy(group, o):
        r = o[1] * nx + o[0]
        at = pl.ds(*groups[group])
        return pltpu.make_async_remote_copy(
            src_ref=ag.at[mxy, at], dst_ref=ag.at[mxy, at],
            send_sem=ag_s.at[group, r], recv_sem=ag_r.at[group, r],
            device_id={"slab": mz * gxy + xy_peer(o)}, device_id_type=MESH)

    hand = pltpu.make_async_remote_copy(
        src_ref=kgs, dst_ref=kgs, send_sem=p_s, recv_sem=p_r,
        device_id={"ex": 1 - ex}, device_id_type=MESH)

    def rs_total(group):
        first_slot, count = groups[group]
        for q in range(first_slot, first_slot + count):
            e, layer = slots[q]
            sources = offs if e == 1 else offs + [(0, 0)]
            for o in sources:
                rs_copy(layer, o, e).wait_recv()
            parts = [rsr[e, layer, o[1] * nx + o[0]] for o in sources]
            if e == 1:
                parts.append(gs[layer, mxy])
            while len(parts) > 1:
                parts = [a + b for a, b in zip(parts[::2], parts[1::2])]
            zr[mz, q] = parts[0]
        for o in zoffs:
            z_copy(group, o).start()

    def z_total(group):
        first_slot, count = groups[group]
        for o in zoffs:
            z_copy(group, o).wait_recv()
        for q in range(first_slot, first_slot + count):
            parts = [zr[i, q] for i in range(nz)]
            while len(parts) > 1:
                parts = [a + b for a, b in zip(parts[::2], parts[1::2])]
            ag[mxy, q] = parts[0]
        for o in offs:
            ag_copy(group, o).start()

    def input_grad():
        for k in range(NC):
            arrive(back_copy, 0, k)
        for r in range(0, H, 8):
            rows = (r, r + 8)
            res = dy[:, flat(*rows)] + back_total(0, rows)
            for i in range(8):
                dx_out[:, r + i, :] = res[:, i * W:(i + 1) * W]

    for k in range(NC):
        arrive(halo_copy, 0, k)
        fill(0, 0, spans(0, k))
        fill(0, 2, spans(0, k))
        layer_one(spans(1, k))
        start(halo_copy, 1, k)
        fill(1, 1, spans(1, k))
    for k in range(NC):
        arrive(halo_copy, 1, k)
        fill(1, 0, spans(1, k))
        fill(1, 2, spans(1, k))
        layer_two(spans(2, k))
        back(1, spans(3, k))
        start(back_copy, 1, k)
    spread(1, weight_grad(1, (0, 16)) + weight_grad(1, (16, H)))
    g1 = None
    for k in range(NC):
        rows = spans(3, k)
        at = flat(*rows)
        arrive(back_copy, 1, k)
        if k == NC - 1:
            rs_start(1)
        dx = dy[:, at] + back_total(1, rows)
        dy[:, at] = dx
        delta = jnp.concatenate([dx * a1[:, at], dx * b1[:, at]], axis=0).astype(BF16)
        store_delta(0, rows, delta)
        if k == 1:
            g1 = weight_grad(0, (0, rows[1]))
        elif k > 1:
            g1 = g1 + weight_grad(0, rows)
    spread(0, g1)
    rs_start(0)
    for r in range(0, H, 16):
        back(0, (r, r + 16))
    for k in range(NC):
        start(back_copy, 0, k)
    bound = 20.0 * float(depth * H * W) ** 0.5
    scaling = float(108 * C * C) ** 0.5 / (bound * 2.0 ** 0.5)

    def factor(e):
        square = None
        for q in range(4):
            if slots[q][0] == e:
                for j in range(16):
                    x = ag[j // tiles, q, j % tiles]
                    square = x * x if square is None else square + x * x
        norm = jnp.sqrt(jnp.sum(square, keepdims=True) + 1e-06)
        return jnp.minimum(1.0, bound / norm)

    @pl.when(ex == 1)
    def _():
        for group in range(2):
            rs_total(group)
        for group in range(2):
            z_total(group)
        input_grad()
        for group in range(2):
            for o in offs:
                ag_copy(group, o).wait_recv()
        factors = factor(0), factor(1)
        for layer in range(2):
            for j in range(16):
                i, n = j // 4, j % 4
                width = min(W, 27 * C - n * W)
                zero, one = ag[j // tiles, 3 - layer, j % tiles], ag[j // tiles, 1 - layer, j % tiles]
                both = (zero * factors[0] + one * factors[1]) * scaling
                kgs[layer, i * 8:(i + 1) * 8, n * W:n * W + width] = both[:, :width]
        hand.start()
        kg_out[...] = kgs[...]
        for group in range(2):
            for o in zoffs:
                z_copy(group, o).wait_send()
            for o in offs:
                ag_copy(group, o).wait_send()
        hand.wait_send()

    @pl.when(ex == 0)
    def _():
        input_grad()
        for layer in range(2):
            rs_copy(layer, (0, 0), 0).wait_send()
        hand.wait_recv()
        kg_out[...] = kgs[...]

    for layer in range(2):
        for o in offs:
            rs_copy(layer, o, ex).wait_send()
        sent(halo_copy, layer)
        sent(back_copy, layer)


def leave(dx_in, kg_in, dx_out, kg_out, sem):
    copies = [pltpu.make_async_copy(a, b, sem.at[i]) for i, (a, b) in enumerate(((dx_in, dx_out), (kg_in, kg_out)))]
    for copy in copies:
        copy.start()
    for copy in copies:
        copy.wait()


def in_hbm(x):
    return pltpu.with_memory_space_constraint(x, pltpu.HBM)


def per_device(volume, cotangent, gate_mask, loss_scale, canary, kernels):
    slabs = lax.axis_size("slab")
    torus = torus_of(slabs)
    nx, ny, nz = torus
    gxy = nx * ny
    part = (16 // gxy, 8, W)
    vm = pl.BlockSpec(memory_space=pltpu.VMEM)
    sm = pl.BlockSpec(memory_space=pltpu.SMEM)
    hbm = pl.BlockSpec(memory_space=pltpu.HBM)
    dma = pltpu.SemaphoreType.DMA
    shapes = (jax.ShapeDtypeStruct((C, H, W), F32), jax.ShapeDtypeStruct((2, 2 * C, 27 * C), F32))
    dx, kg = pl.pallas_call(
        functools.partial(kernel, torus, slabs),
        out_shape=shapes,
        in_specs=[hbm, hbm, hbm, sm, sm, hbm],
        out_specs=(vm, vm),
        scratch_shapes=[
            pltpu.VMEM((C, H, W), BF16),
            pltpu.VMEM((C, H, W), BF16),
            pltpu.VMEM((2, H, W), jnp.int32),
            pltpu.VMEM((2, 2 * C, 27 * C), BF16),
            pltpu.VMEM((C, H, W), F32),
            pltpu.VMEM((2, 9, C, PW), BF16),
            pltpu.VMEM((2, 3, 2 * C, PW), BF16),
            pltpu.VMEM((18 * C, W), F32),
            pltpu.VMEM((2, 3 * C, 18 * C), BF16),
            pltpu.VMEM((2, C, H * W), F32),
            pltpu.VMEM((C, H * W), F32),
            pltpu.VMEM((C, H * W), F32),
            pltpu.VMEM((C, H * W), F32),
            pltpu.VMEM((C, H * W), F32),
            pltpu.VMEM((2, 2, C, H * W), BF16),
            pltpu.VMEM((2, 2, C, H * W), BF16),
            pltpu.VMEM((2, 2 * C, 4 * W), F32),
            pltpu.VMEM((2, gxy) + part, F32),
            pltpu.VMEM((2, 2, gxy) + part, F32),
            pltpu.VMEM((nz, 4) + part, F32),
            pltpu.VMEM((gxy, 4) + part, F32),
            pltpu.VMEM((2, 2 * C, 27 * C), F32),
            dma((2, 2, NC)), dma((2, 2, NC)), dma((2, 2, NC)), dma((2, 2, NC)),
            dma((2, gxy)), dma((2, 2, gxy)), dma((2, nz)), dma((2, nz)), dma((2, gxy)), dma((2, gxy)),
            dma, dma, dma((4,)),
        ],
        compiler_params=pltpu.CompilerParams(
            collective_id=0, has_side_effects=True, vmem_limit_bytes=48 * 1024 * 1024),
        name="gated_level",
    )(
        in_hbm(volume.reshape((C, H, W))),
        in_hbm(cotangent.reshape((C, H, W))),
        in_hbm(gate_mask.reshape((2, H, W))),
        loss_scale,
        canary,
        in_hbm(kernels),
    )
    dx, kg = pl.pallas_call(
        leave,
        out_shape=shapes,
        in_specs=[vm, vm],
        out_specs=(hbm, hbm),
        scratch_shapes=[dma((2,))],
        compiler_params=pltpu.CompilerParams(vmem_limit_bytes=1024 * 1024),
        name="leave",
    )(dx, kg)
    return dx.reshape((1, C, 1, H, W)), kg


def solution(mesh):
    placed = (
        P("ex", None, "slab", None, None),
        P("ex", None, "slab", None, None),
        P("ex", None, "slab", None, None),
        P("ex"),
        P("ex"),
        P(),
    )
    return jax.shard_map(
        per_device,
        mesh=mesh,
        in_specs=placed,
        out_specs=(P("ex", None, "slab", None, None), P()),
        check_vma=False,
    )
```

time: 56 us -> 50.3 us (0.90)
  local copies, waits for them, and re-layouts: 4.76 us -> 0 us
  Pallas kernels: 49 us -> 48.3 us
    unnamed x10 -> x0, local copies, waits for them, and re-layouts: 4.76 us -> none
    pallas_call x1 -> x2, Pallas kernels: 49 us -> 48.3 us  [the longest x1 47.5 us: per_device(): pl.pallas_call(functools.partial(kernel, torus, slabs), out_shape=shapes,...]
where the time goes in v2:
time: 50.3 us; the launch traced here: 50.2 us
  Pallas kernels  48.3 us (96%)
  between operations  1.93 us (4%)
    pallas_call x1, Pallas kernels, per_device(): pl.pallas_call(functools.partial(kernel, torus, slabs), out_shape=shapes,...  47.5 us

profile of v2, /device:TPU:1, one launch (start us, length us, event | category | flops | bytes accessed | tf_op | source)
XLA Modules:
  0.0 50.2 jit_solution(17927584091999898659)
XLA Ops:
  1.9 47.5 %gated_level.1 = (f32[16,32,128]{2,1,0:T(8,128)S(1)}, f32[2,32,432]{2,1,0:T(8,128)S(1)}) custom-call(bf16[16,32,128]{2,1,0:T(8,128)(2,1)} %bitcast.6, bf16[16,32,128]{2,1,0:T(8,128)(2,1)} %bitcast.7, s32[2,32,128]{2,1,0:T(8,128)} %bitcast.8, f32[1]{0:T(128)S(6)} %copy.9.scale, s32[1]{0:T(128)S(6)} %copy.10.canary, bf16[2,32,432]{2,1,0:T(8,128)(2,1)} %ker_hbm.1), custom_call_target="tpu_custom_call" | custom-call | tf_op jit(solution)/shard_map/gated_level/pallas_call | solution.py:452
  49.5 0.8 %leave.1 = (f32[16,32,128]{2,1,0:T(8,128)}, f32[2,32,432]{2,1,0:T(8,128)}) custom-call(f32[16,32,128]{2,1,0:T(8,128)S(1)} %get-tuple-element.6.dx_in, f32[2,32,432]{2,1,0:T(8,128)S(1)} %get-tuple-element.7.kg_in), custom_call_target="tpu_custom_call" | custom-call | tf_op jit(solution)/shard_map/leave/pallas_call | solution.py:495

commit v3 on v2

--- a/solution.py
+++ b/solution.py
@@ -133,14 +133,14 @@
         at = flat(1 + r0, 1 + r1)
         return pltpu.make_async_remote_copy(
             src_ref=xb.at[layer, 4, :, at], dst_ref=xb.at[layer, 6 * side + 1, :, at],
-            send_sem=xs_sem.at[layer, side, k], recv_sem=xr_sem.at[layer, side, k],
+            send_sem=xs_sem.at[layer, side], recv_sem=xr_sem.at[layer, side, k],
             device_id={"slab": (up, down)[side]}, device_id_type=MESH)
 
     def back_copy(layer, side, k):
-        at = flat(*spans(3, k))
+        at = flat(0, H) if layer == 0 else flat(*spans(3, k))
         return pltpu.make_async_remote_copy(
             src_ref=bsend.at[layer, side, :, at], dst_ref=brecv.at[layer, side, :, at],
-            send_sem=bs_sem.at[layer, side, k], recv_sem=br_sem.at[layer, side, k],
+            send_sem=bs_sem.at[layer, side], recv_sem=br_sem.at[side, NC if layer == 0 else k],
             device_id={"slab": (up, down)[side]}, device_id_type=MESH)
 
     def start(copy, layer, k):
@@ -161,16 +161,14 @@
         def _():
             copy(layer, 1, k).wait_recv()
 
-    def sent(copy, layer):
-        @pl.when(has_up)
-        def _():
-            for k in range(NC):
-                copy(layer, 0, k).wait_send()
-
-        @pl.when(has_down)
-        def _():
-            for k in range(NC):
-                copy(layer, 1, k).wait_send()
+    def sent(layer):
+        for side, there in ((0, has_up), (1, has_down)):
+            @pl.when(there)
+            def _():
+                for ref, sem in ((xb.at[layer, 4, :, flat(1, 1 + H)], xs_sem), (bsend.at[layer, side], bs_sem)):
+                    pltpu.make_async_remote_copy(
+                        src_ref=ref, dst_ref=ref, send_sem=sem.at[layer, side], recv_sem=br_sem.at[side, 0],
+                        device_id={"slab": (up, down)[side]}, device_id_type=MESH).wait_send()
 
     def store_delta(layer, rows, delta):
         for i, r in enumerate(range(*rows)):
@@ -263,12 +261,17 @@
             i, n = j // 4, j % 4
             gs[layer, j // tiles, j % tiles] = gpad[layer, i * 8:(i + 1) * 8, n * W:(n + 1) * W]
 
+    def tally(ref, send_sem, recv_sem):
+        return pltpu.make_async_remote_copy(
+            src_ref=ref, dst_ref=ref, send_sem=send_sem, recv_sem=recv_sem,
+            device_id={"ex": 1 - ex}, device_id_type=MESH)
+
     def rs_copy(layer, o, e):
         r = o[1] * nx + o[0]
         peer = xy_peer(o)
         return pltpu.make_async_remote_copy(
             src_ref=gs.at[layer, peer], dst_ref=rsr.at[e, layer, r],
-            send_sem=rs_s.at[layer, r], recv_sem=rs_r.at[e, layer, r],
+            send_sem=rs_s.at[layer], recv_sem=rs_r.at[e, layer],
             device_id={"ex": 1, "slab": mz * gxy + peer}, device_id_type=MESH)
 
     def rs_start(layer):
@@ -283,29 +286,32 @@
         at = pl.ds(*groups[group])
         return pltpu.make_async_remote_copy(
             src_ref=zr.at[mz, at], dst_ref=zr.at[mz, at],
-            send_sem=z_s.at[group, o], recv_sem=z_r.at[group, o],
+            send_sem=z_s.at[group], recv_sem=z_r.at[group],
             device_id={"slab": lax.rem(mz + o, nz) * gxy + mxy}, device_id_type=MESH)
 
+    def z_all(group):
+        return tally(zr.at[pl.ds(1, nz - 1), pl.ds(*groups[group])], z_s.at[group], z_r.at[group])
+
+    def ag_all(group):
+        return tally(ag.at[pl.ds(1, gxy - 1), pl.ds(*groups[group])], ag_s.at[group], ag_r.at[group])
+
     def ag_copy(group, o):
-        r = o[1] * nx + o[0]
         at = pl.ds(*groups[group])
         return pltpu.make_async_remote_copy(
             src_ref=ag.at[mxy, at], dst_ref=ag.at[mxy, at],
-            send_sem=ag_s.at[group, r], recv_sem=ag_r.at[group, r],
+            send_sem=ag_s.at[group], recv_sem=ag_r.at[group],
             device_id={"slab": mz * gxy + xy_peer(o)}, device_id_type=MESH)
 
     hand = pltpu.make_async_remote_copy(
-        src_ref=kgs, dst_ref=kgs, send_sem=p_s, recv_sem=p_r,
+        src_ref=kgs, dst_ref=kg_out, send_sem=p_s, recv_sem=p_r,
         device_id={"ex": 1 - ex}, device_id_type=MESH)
 
     def rs_total(group):
         first_slot, count = groups[group]
         for q in range(first_slot, first_slot + count):
             e, layer = slots[q]
-            sources = offs if e == 1 else offs + [(0, 0)]
-            for o in sources:
-                rs_copy(layer, o, e).wait_recv()
-            parts = [rsr[e, layer, o[1] * nx + o[0]] for o in sources]
+            tally(rsr.at[e, layer, pl.ds(e, gxy - e)], rs_s.at[layer], rs_r.at[e, layer]).wait_recv()
+            parts = [rsr[e, layer, r] for r in range(e, gxy)]
             if e == 1:
                 parts.append(gs[layer, mxy])
             while len(parts) > 1:
@@ -316,8 +322,7 @@
 
     def z_total(group):
         first_slot, count = groups[group]
-        for o in zoffs:
-            z_copy(group, o).wait_recv()
+        z_all(group).wait_recv()
         for q in range(first_slot, first_slot + count):
             parts = [zr[i, q] for i in range(nz)]
             while len(parts) > 1:
@@ -326,14 +331,17 @@
         for o in offs:
             ag_copy(group, o).start()
 
+    dx_copy = pltpu.make_async_copy(tmp, dx_out, in_sem.at[0])
+    kg_copy = pltpu.make_async_copy(kgs, kg_out, in_sem.at[1])
+
     def input_grad():
-        for k in range(NC):
-            arrive(back_copy, 0, k)
+        arrive(back_copy, 0, 0)
         for r in range(0, H, 8):
             rows = (r, r + 8)
             res = dy[:, flat(*rows)] + back_total(0, rows)
             for i in range(8):
-                dx_out[:, r + i, :] = res[:, i * W:(i + 1) * W]
+                tmp[:, r + i, :] = res[:, i * W:(i + 1) * W]
+        dx_copy.start()
 
     for k in range(NC):
         arrive(halo_copy, 0, k)
@@ -355,22 +363,19 @@
         rows = spans(3, k)
         at = flat(*rows)
         arrive(back_copy, 1, k)
-        if k == NC - 1:
-            rs_start(1)
         dx = dy[:, at] + back_total(1, rows)
         dy[:, at] = dx
         delta = jnp.concatenate([dx * a1[:, at], dx * b1[:, at]], axis=0).astype(BF16)
         store_delta(0, rows, delta)
-        if k == 1:
-            g1 = weight_grad(0, (0, rows[1]))
-        elif k > 1:
-            g1 = g1 + weight_grad(0, rows)
+        part = weight_grad(0, rows)
+        g1 = part if k == 0 else g1 + part
+        if k == NC - 2:
+            rs_start(1)
     spread(0, g1)
     rs_start(0)
     for r in range(0, H, 16):
         back(0, (r, r + 16))
-    for k in range(NC):
-        start(back_copy, 0, k)
+    start(back_copy, 0, 0)
     bound = 20.0 * float(depth * H * W) ** 0.5
     scaling = float(108 * C * C) ** 0.5 / (bound * 2.0 ** 0.5)
 
@@ -392,8 +397,7 @@
             z_total(group)
         input_grad()
         for group in range(2):
-            for o in offs:
-                ag_copy(group, o).wait_recv()
+            ag_all(group).wait_recv()
         factors = factor(0), factor(1)
         for layer in range(2):
             for j in range(16):
@@ -403,27 +407,25 @@
                 both = (zero * factors[0] + one * factors[1]) * scaling
                 kgs[layer, i * 8:(i + 1) * 8, n * W:n * W + width] = both[:, :width]
         hand.start()
-        kg_out[...] = kgs[...]
+        kg_copy.start()
+        for layer in range(2):
+            tally(gs.at[layer, pl.ds(1, gxy - 1)], rs_s.at[layer], rs_r.at[1, layer]).wait_send()
         for group in range(2):
-            for o in zoffs:
-                z_copy(group, o).wait_send()
-            for o in offs:
-                ag_copy(group, o).wait_send()
+            z_all(group).wait_send()
+            ag_all(group).wait_send()
         hand.wait_send()
+        kg_copy.wait()
 
     @pl.when(ex == 0)
     def _():
         input_grad()
         for layer in range(2):
-            rs_copy(layer, (0, 0), 0).wait_send()
+            tally(gs.at[layer], rs_s.at[layer], rs_r.at[0, layer]).wait_send()
         hand.wait_recv()
-        kg_out[...] = kgs[...]
-
+
+    dx_copy.wait()
     for layer in range(2):
-        for o in offs:
-            rs_copy(layer, o, ex).wait_send()
-        sent(halo_copy, layer)
-        sent(back_copy, layer)
+        sent(layer)
 
 
 def leave(dx_in, kg_in, dx_out, kg_out, sem):
@@ -444,16 +446,16 @@
     nx, ny, nz = torus
     gxy = nx * ny
     part = (16 // gxy, 8, W)
-    vm = pl.BlockSpec(memory_space=pltpu.VMEM)
     sm = pl.BlockSpec(memory_space=pltpu.SMEM)
     hbm = pl.BlockSpec(memory_space=pltpu.HBM)
+    anywhere = pl.BlockSpec(memory_space=pl.ANY)
     dma = pltpu.SemaphoreType.DMA
     shapes = (jax.ShapeDtypeStruct((C, H, W), F32), jax.ShapeDtypeStruct((2, 2 * C, 27 * C), F32))
     dx, kg = pl.pallas_call(
         functools.partial(kernel, torus, slabs),
         out_shape=shapes,
         in_specs=[hbm, hbm, hbm, sm, sm, hbm],
-        out_specs=(vm, vm),
+        out_specs=(anywhere, anywhere),
         scratch_shapes=[
             pltpu.VMEM((C, H, W), BF16),
             pltpu.VMEM((C, H, W), BF16),
@@ -477,8 +479,8 @@
             pltpu.VMEM((nz, 4) + part, F32),
             pltpu.VMEM((gxy, 4) + part, F32),
             pltpu.VMEM((2, 2 * C, 27 * C), F32),
-            dma((2, 2, NC)), dma((2, 2, NC)), dma((2, 2, NC)), dma((2, 2, NC)),
-            dma((2, gxy)), dma((2, 2, gxy)), dma((2, nz)), dma((2, nz)), dma((2, gxy)), dma((2, gxy)),
+            dma((2, 2)), dma((2, 2, NC)), dma((2, 2)), dma((2, NC + 1)),
+            dma((2,)), dma((2, 2)), dma((2,)), dma((2,)), dma((2,)), dma((2,)),
             dma, dma, dma((4,)),
         ],
         compiler_params=pltpu.CompilerParams(
@@ -495,7 +497,7 @@
     dx, kg = pl.pallas_call(
         leave,
         out_shape=shapes,
-        in_specs=[vm, vm],
+        in_specs=[anywhere, anywhere],
         out_specs=(hbm, hbm),
         scratch_shapes=[dma((2,))],
         compiler_params=pltpu.CompilerParams(vmem_limit_bytes=1024 * 1024),

time: 50.3 us -> 47.7 us (0.948)
  Pallas kernels: 48.3 us -> 45.7 us
    pallas_call x1, Pallas kernels: 47.5 us -> 44.9 us  [per_device(): pl.pallas_call(functools.partial(kernel, torus, slabs), out_shape=shapes,...]
where the time goes in v3:
time: 47.7 us; the launch traced here: 47.6 us
  Pallas kernels  45.7 us (96%)
  between operations  1.93 us (4%)
    pallas_call x1, Pallas kernels, per_device(): pl.pallas_call(functools.partial(kernel, torus, slabs), out_shape=shapes,...  44.9 us

profile of v3, /device:TPU:1, one launch (start us, length us, event | category | flops | bytes accessed | tf_op | source)
XLA Modules:
  0.0 47.6 jit_solution(15803794779637107157)
XLA Ops:
  1.9 44.9 %gated_level.1 = (f32[16,32,128]{2,1,0:T(8,128)S(1)}, f32[2,32,432]{2,1,0:T(8,128)S(1)}) custom-call(bf16[16,32,128]{2,1,0:T(8,128)(2,1)} %bitcast.6, bf16[16,32,128]{2,1,0:T(8,128)(2,1)} %bitcast.7, s32[2,32,128]{2,1,0:T(8,128)} %bitcast.8, f32[1]{0:T(128)S(6)} %copy.9.scale, s32[1]{0:T(128)S(6)} %copy.10.canary, bf16[2,32,432]{2,1,0:T(8,128)(2,1)} %ker_hbm.1), custom_call_target="tpu_custom_call" | custom-call | tf_op jit(solution)/shard_map/gated_level/pallas_call | solution.py:454
  46.8 0.8 %leave.1 = (f32[16,32,128]{2,1,0:T(8,128)}, f32[2,32,432]{2,1,0:T(8,128)}) custom-call(f32[16,32,128]{2,1,0:T(8,128)S(1)} %get-tuple-element.6.dx_in, f32[2,32,432]{2,1,0:T(8,128)S(1)} %get-tuple-element.7.kg_in), custom_call_target="tpu_custom_call" | custom-call | tf_op jit(solution)/shard_map/leave/pallas_call | solution.py:497

commit v4 on v3

--- a/solution.py
+++ b/solution.py
@@ -14,10 +14,10 @@
 W = 128
 PW = (H + 2) * W
 ROWS = (
-    (0, 10, 20, 28, 32),
-    (0, 9, 19, 27, 32),
-    (0, 8, 18, 26, 32),
-    (0, 7, 17, 25, 32),
+    (0, 8, 16, 23, 29, 32),
+    (0, 7, 15, 22, 28, 32),
+    (0, 6, 14, 21, 27, 32),
+    (0, 5, 13, 20, 26, 32),
 )
 NC = len(ROWS[0]) - 1
 
@@ -26,6 +26,10 @@
     return {128: (4, 4, 8), 8: (2, 2, 2)}[slabs]
 
 
+def owners_of(slabs):
+    return {128: tuple((x, y) for y in range(4) for x in range(4)), 8: ((0, 0), (1, 0), (0, 1), (1, 1))}[slabs]
+
+
 def spans(stage, k):
     return ROWS[stage][k], ROWS[stage][k + 1]
 
@@ -36,7 +40,7 @@
 
 def kernel(torus, depth, vol_hbm, cot_hbm, mask_hbm, scale, canary, ker_hbm, dx_out, kg_out,
            vol, cot, mask, ker, tmp, xb, db, kbt, kb, mk, a1, b1, dy, own, bsend, brecv, gpad,
-           gs, rsr, zr, ag, kgs,
+           gs, rsr, zr, ag,
            xs_sem, xr_sem, bs_sem, br_sem, rs_s, rs_r, z_s, z_r, ag_s, ag_r, p_s, p_r, in_sem):
     nx, ny, nz = torus
     gxy = nx * ny
@@ -50,9 +54,15 @@
     offs = [(a, b) for b in range(ny) for a in range(nx) if (a, b) != (0, 0)]
     offs.sort(key=lambda o: -(min(o[0], nx - o[0]) + min(o[1], ny - o[1])))
     zoffs = sorted(range(1, nz), key=lambda o: -min(o, nz - o))
-    tiles = 16 // gxy
-    slots = ((1, 1), (1, 0), (0, 1), (0, 0))
-    groups = ((0, 3), (3, 1))
+    owners = owners_of(slabs)
+    held = len(owners)
+    tiles = 16 // held
+    slots = ((1, 1), (0, 1), (1, 0), (0, 0))
+    groups = ((0, 2), (2, 1), (3, 1))
+    mine = [((mx == a) & (my == b)).astype(jnp.int32) for a, b in owners]
+    owns = sum(mine)
+    mo = sum(i * m for i, m in enumerate(mine))
+    is_owner = owns > 0
     has_down = me > 0
     has_up = me < slabs - 1
     up = jnp.minimum(me + 1, slabs - 1)
@@ -74,13 +84,18 @@
     def _():
         signal({"slab": down})
 
-    @pl.when(ex == 1)
+    @pl.when((ex == 1) & is_owner)
     def _():
         for o in offs:
             for e in range(2):
                 signal({"ex": e, "slab": mz * gxy + xy_peer(o)})
         for o in zoffs:
             signal({"slab": lax.rem(mz + o, nz) * gxy + mxy})
+
+    @pl.when((ex == 1) & jnp.logical_not(is_owner))
+    def _():
+        for a, b in owners:
+            signal({"slab": mz * gxy + b * nx + a})
 
     signal({"ex": 1 - ex})
     loads = [pltpu.make_async_copy(src, dst, in_sem.at[q]) for q, (src, dst) in enumerate(
@@ -91,14 +106,16 @@
     first = lane == 0
     last = lane == W - 1
 
+    keep_right = jnp.where(first, 0.0, 1.0).astype(BF16)
+    keep_left = jnp.where(last, 0.0, 1.0).astype(BF16)
+
     def shifts(x):
-        rows = x.shape[0] // C
         left, right = [], []
-        for i in range(rows):
-            part = x[i * C:(i + 1) * C, :].astype(F32)
-            left.append(jnp.where(first, 0.0, pltpu.roll(part, 1, 1)).astype(BF16))
-            right.append(jnp.where(last, 0.0, pltpu.roll(part, W - 1, 1)).astype(BF16))
-        if rows == 1:
+        for i in range(x.shape[0] // C):
+            part = x[i * C:(i + 1) * C, :]
+            left.append(pltpu.roll(part, 1, 1) * keep_right)
+            right.append(pltpu.roll(part, W - 1, 1) * keep_left)
+        if len(left) == 1:
             return left[0], right[0]
         return jnp.concatenate(left, axis=0), jnp.concatenate(right, axis=0)
 
@@ -210,7 +227,8 @@
                 db[layer, q, :C, at] = zero_row
                 db[layer, q, C:, at] = zero_row
     gpad[...] = jnp.zeros_like(gpad)
-    many = jnp.where(ex == 1, len(offs) + len(zoffs) + 1, len(offs) + 1)
+    many = 1 + jnp.where(
+        ex == 1, jnp.where(is_owner, len(offs) + len(zoffs), held), held - owns)
     pl.semaphore_wait(barrier, many + has_up.astype(jnp.int32) + has_down.astype(jnp.int32))
     for k in range(NC):
         start(halo_copy, 0, k)
@@ -266,21 +284,16 @@
             src_ref=ref, dst_ref=ref, send_sem=send_sem, recv_sem=recv_sem,
             device_id={"ex": 1 - ex}, device_id_type=MESH)
 
-    def rs_copy(layer, o, e):
-        r = o[1] * nx + o[0]
-        peer = xy_peer(o)
-        return pltpu.make_async_remote_copy(
-            src_ref=gs.at[layer, peer], dst_ref=rsr.at[e, layer, r],
-            send_sem=rs_s.at[layer], recv_sem=rs_r.at[e, layer],
-            device_id={"ex": 1, "slab": mz * gxy + peer}, device_id_type=MESH)
-
     def rs_start(layer):
-        for o in offs:
-            rs_copy(layer, o, ex).start()
-
-        @pl.when(ex == 0)
-        def _():
-            rs_copy(layer, (0, 0), 0).start()
+        for i, (a, b) in enumerate(owners):
+            copy = pltpu.make_async_remote_copy(
+                src_ref=gs.at[layer, i], dst_ref=rsr.at[ex, layer, mxy],
+                send_sem=rs_s.at[layer], recv_sem=rs_r.at[ex, layer],
+                device_id={"ex": 1, "slab": mz * gxy + b * nx + a}, device_id_type=MESH)
+
+            @pl.when((ex == 0) | (mine[i] == 0))
+            def _():
+                copy.start()
 
     def z_copy(group, o):
         at = pl.ds(*groups[group])
@@ -292,28 +305,28 @@
     def z_all(group):
         return tally(zr.at[pl.ds(1, nz - 1), pl.ds(*groups[group])], z_s.at[group], z_r.at[group])
 
-    def ag_all(group):
-        return tally(ag.at[pl.ds(1, gxy - 1), pl.ds(*groups[group])], ag_s.at[group], ag_r.at[group])
+    def ag_all(group, count):
+        return tally(ag.at[pl.ds(0, count), pl.ds(*groups[group])], ag_s.at[group], ag_r.at[group])
 
     def ag_copy(group, o):
         at = pl.ds(*groups[group])
         return pltpu.make_async_remote_copy(
-            src_ref=ag.at[mxy, at], dst_ref=ag.at[mxy, at],
+            src_ref=ag.at[mo, at], dst_ref=ag.at[mo, at],
             send_sem=ag_s.at[group], recv_sem=ag_r.at[group],
             device_id={"slab": mz * gxy + xy_peer(o)}, device_id_type=MESH)
 
     hand = pltpu.make_async_remote_copy(
-        src_ref=kgs, dst_ref=kg_out, send_sem=p_s, recv_sem=p_r,
+        src_ref=kg_out, dst_ref=kg_out, send_sem=p_s, recv_sem=p_r,
         device_id={"ex": 1 - ex}, device_id_type=MESH)
 
     def rs_total(group):
         first_slot, count = groups[group]
         for q in range(first_slot, first_slot + count):
             e, layer = slots[q]
+            if e == 1:
+                rsr[1, layer, mxy] = gs[layer, mo]
             tally(rsr.at[e, layer, pl.ds(e, gxy - e)], rs_s.at[layer], rs_r.at[e, layer]).wait_recv()
-            parts = [rsr[e, layer, r] for r in range(e, gxy)]
-            if e == 1:
-                parts.append(gs[layer, mxy])
+            parts = [rsr[e, layer, r] for r in range(gxy)]
             while len(parts) > 1:
                 parts = [a + b for a, b in zip(parts[::2], parts[1::2])]
             zr[mz, q] = parts[0]
@@ -327,12 +340,9 @@
             parts = [zr[i, q] for i in range(nz)]
             while len(parts) > 1:
                 parts = [a + b for a, b in zip(parts[::2], parts[1::2])]
-            ag[mxy, q] = parts[0]
+            ag[mo, q] = parts[0]
         for o in offs:
             ag_copy(group, o).start()
-
-    dx_copy = pltpu.make_async_copy(tmp, dx_out, in_sem.at[0])
-    kg_copy = pltpu.make_async_copy(kgs, kg_out, in_sem.at[1])
 
     def input_grad():
         arrive(back_copy, 0, 0)
@@ -340,8 +350,7 @@
             rows = (r, r + 8)
             res = dy[:, flat(*rows)] + back_total(0, rows)
             for i in range(8):
-                tmp[:, r + i, :] = res[:, i * W:(i + 1) * W]
-        dx_copy.start()
+                dx_out[:, r + i, :] = res[:, i * W:(i + 1) * W]
 
     for k in range(NC):
         arrive(halo_copy, 0, k)
@@ -349,7 +358,7 @@
         fill(0, 2, spans(0, k))
         layer_one(spans(1, k))
         start(halo_copy, 1, k)
-        fill(1, 1, spans(1, k))
+    fill(1, 1, (0, H))
     for k in range(NC):
         arrive(halo_copy, 1, k)
         fill(1, 0, spans(1, k))
@@ -389,32 +398,50 @@
         norm = jnp.sqrt(jnp.sum(square, keepdims=True) + 1e-06)
         return jnp.minimum(1.0, bound / norm)
 
+    @pl.when((ex == 1) & is_owner)
+    def _():
+        for group in range(len(groups)):
+            rs_total(group)
+        for group in range(len(groups)):
+            z_total(group)
+
     @pl.when(ex == 1)
     def _():
-        for group in range(2):
-            rs_total(group)
-        for group in range(2):
-            z_total(group)
         input_grad()
-        for group in range(2):
-            ag_all(group).wait_recv()
+
+        @pl.when(is_owner)
+        def _():
+            for group in range(len(groups)):
+                ag_all(group, held - 1).wait_recv()
+
+        @pl.when(jnp.logical_not(is_owner))
+        def _():
+            for group in range(len(groups)):
+                ag_all(group, held).wait_recv()
+
         factors = factor(0), factor(1)
         for layer in range(2):
             for j in range(16):
                 i, n = j // 4, j % 4
                 width = min(W, 27 * C - n * W)
-                zero, one = ag[j // tiles, 3 - layer, j % tiles], ag[j // tiles, 1 - layer, j % tiles]
+                zero, one = (ag[j // tiles, slots.index((e, layer)), j % tiles] for e in range(2))
                 both = (zero * factors[0] + one * factors[1]) * scaling
-                kgs[layer, i * 8:(i + 1) * 8, n * W:n * W + width] = both[:, :width]
+                kg_out[layer, i * 8:(i + 1) * 8, n * W:n * W + width] = both[:, :width]
         hand.start()
-        kg_copy.start()
-        for layer in range(2):
-            tally(gs.at[layer, pl.ds(1, gxy - 1)], rs_s.at[layer], rs_r.at[1, layer]).wait_send()
-        for group in range(2):
-            z_all(group).wait_send()
-            ag_all(group).wait_send()
+        @pl.when(is_owner)
+        def _():
+            for layer in range(2):
+                tally(gs.at[layer, pl.ds(1, held - 1)], rs_s.at[layer], rs_r.at[1, layer]).wait_send()
+            for group in range(len(groups)):
+                z_all(group).wait_send()
+                tally(ag.at[pl.ds(0, gxy - 1), pl.ds(*groups[group])], ag_s.at[group], ag_r.at[group]).wait_send()
+
+        @pl.when(jnp.logical_not(is_owner))
+        def _():
+            for layer in range(2):
+                tally(gs.at[layer], rs_s.at[layer], rs_r.at[1, layer]).wait_send()
+
         hand.wait_send()
-        kg_copy.wait()
 
     @pl.when(ex == 0)
     def _():
@@ -423,7 +450,6 @@
             tally(gs.at[layer], rs_s.at[layer], rs_r.at[0, layer]).wait_send()
         hand.wait_recv()
 
-    dx_copy.wait()
     for layer in range(2):
         sent(layer)
 
@@ -445,17 +471,19 @@
     torus = torus_of(slabs)
     nx, ny, nz = torus
     gxy = nx * ny
-    part = (16 // gxy, 8, W)
+    held = len(owners_of(slabs))
+    part = (16 // held, 8, W)
     sm = pl.BlockSpec(memory_space=pltpu.SMEM)
     hbm = pl.BlockSpec(memory_space=pltpu.HBM)
     anywhere = pl.BlockSpec(memory_space=pl.ANY)
+    vm = pl.BlockSpec(memory_space=pltpu.VMEM)
     dma = pltpu.SemaphoreType.DMA
     shapes = (jax.ShapeDtypeStruct((C, H, W), F32), jax.ShapeDtypeStruct((2, 2 * C, 27 * C), F32))
     dx, kg = pl.pallas_call(
         functools.partial(kernel, torus, slabs),
         out_shape=shapes,
         in_specs=[hbm, hbm, hbm, sm, sm, hbm],
-        out_specs=(anywhere, anywhere),
+        out_specs=(vm, vm),
         scratch_shapes=[
             pltpu.VMEM((C, H, W), BF16),
             pltpu.VMEM((C, H, W), BF16),
@@ -474,13 +502,12 @@
             pltpu.VMEM((2, 2, C, H * W), BF16),
             pltpu.VMEM((2, 2, C, H * W), BF16),
             pltpu.VMEM((2, 2 * C, 4 * W), F32),
-            pltpu.VMEM((2, gxy) + part, F32),
+            pltpu.VMEM((2, held) + part, F32),
             pltpu.VMEM((2, 2, gxy) + part, F32),
             pltpu.VMEM((nz, 4) + part, F32),
-            pltpu.VMEM((gxy, 4) + part, F32),
-            pltpu.VMEM((2, 2 * C, 27 * C), F32),
+            pltpu.VMEM((held, 4) + part, F32),
             dma((2, 2)), dma((2, 2, NC)), dma((2, 2)), dma((2, NC + 1)),
-            dma((2,)), dma((2, 2)), dma((2,)), dma((2,)), dma((2,)), dma((2,)),
+            dma((2,)), dma((2, 2)), dma((3,)), dma((3,)), dma((3,)), dma((3,)),
             dma, dma, dma((4,)),
         ],
         compiler_params=pltpu.CompilerParams(

time: 47.7 us -> 47.1 us (0.987)
  Pallas kernels: 45.7 us -> 45.1 us
    pallas_call x1, Pallas kernels: 44.9 us -> 44.3 us  [per_device(): pl.pallas_call(functools.partial(kernel, torus, slabs), out_shape=shapes,...]
where the time goes in v4:
time: 47.1 us; the launch traced here: 47 us
  Pallas kernels  45.1 us (96%)
  between operations  1.93 us (4%)
    pallas_call x1, Pallas kernels, per_device(): pl.pallas_call(functools.partial(kernel, torus, slabs), out_shape=shapes,...  44.3 us

profile of v4, /device:TPU:1, one launch (start us, length us, event | category | flops | bytes accessed | tf_op | source)
XLA Modules:
  0.0 47.0 jit_solution(13139621284825749233)
XLA Ops:
  1.9 44.3 %gated_level.1 = (f32[16,32,128]{2,1,0:T(8,128)S(1)}, f32[2,32,432]{2,1,0:T(8,128)S(1)}) custom-call(bf16[16,32,128]{2,1,0:T(8,128)(2,1)} %bitcast.6, bf16[16,32,128]{2,1,0:T(8,128)(2,1)} %bitcast.7, s32[2,32,128]{2,1,0:T(8,128)} %bitcast.8, f32[1]{0:T(128)S(6)} %copy.9.scale, s32[1]{0:T(128)S(6)} %copy.10.canary, bf16[2,32,432]{2,1,0:T(8,128)(2,1)} %ker_hbm.1), custom_call_target="tpu_custom_call" | custom-call | tf_op jit(solution)/shard_map/gated_level/pallas_call | solution.py:482
  46.2 0.8 %leave.1 = (f32[16,32,128]{2,1,0:T(8,128)}, f32[2,32,432]{2,1,0:T(8,128)}) custom-call(f32[16,32,128]{2,1,0:T(8,128)S(1)} %get-tuple-element.6.dx_in, f32[2,32,432]{2,1,0:T(8,128)S(1)} %get-tuple-element.7.kg_in), custom_call_target="tpu_custom_call" | custom-call | tf_op jit(solution)/shard_map/leave/pallas_call | solution.py:524

commit v5 on v4

--- a/solution.py
+++ b/solution.py
@@ -285,15 +285,18 @@
             device_id={"ex": 1 - ex}, device_id_type=MESH)
 
     def rs_start(layer):
-        for i, (a, b) in enumerate(owners):
-            copy = pltpu.make_async_remote_copy(
-                src_ref=gs.at[layer, i], dst_ref=rsr.at[ex, layer, mxy],
+        def to(peer):
+            return pltpu.make_async_remote_copy(
+                src_ref=gs.at[layer, peer], dst_ref=rsr.at[ex, layer, mxy],
                 send_sem=rs_s.at[layer], recv_sem=rs_r.at[ex, layer],
-                device_id={"ex": 1, "slab": mz * gxy + b * nx + a}, device_id_type=MESH)
-
-            @pl.when((ex == 0) | (mine[i] == 0))
-            def _():
-                copy.start()
+                device_id={"ex": 1, "slab": mz * gxy + peer}, device_id_type=MESH)
+
+        for o in offs:
+            to(xy_peer(o)).start()
+
+        @pl.when(ex == 0)
+        def _():
+            to(mxy).start()
 
     def z_copy(group, o):
         at = pl.ds(*groups[group])
@@ -375,13 +378,18 @@
         dx = dy[:, at] + back_total(1, rows)
         dy[:, at] = dx
         delta = jnp.concatenate([dx * a1[:, at], dx * b1[:, at]], axis=0).astype(BF16)
-        store_delta(0, rows, delta)
+        db[0, 1, :, flat(1 + rows[0], 1 + rows[1])] = delta
         part = weight_grad(0, rows)
         g1 = part if k == 0 else g1 + part
-        if k == NC - 2:
+        if k == 1:
             rs_start(1)
     spread(0, g1)
     rs_start(0)
+    for r in range(H):
+        at = flat(1 + r, 2 + r)
+        left, right = shifts(db[0, 1, :, at])
+        db[0, 2, :, at] = left
+        db[0, 0, :, at] = right
     for r in range(0, H, 16):
         back(0, (r, r + 16))
     start(back_copy, 0, 0)

time: 47.1 us -> 46.5 us (0.987)
  Pallas kernels: 45.1 us -> 44.5 us
    pallas_call x1, Pallas kernels: 44.3 us -> 43.7 us  [per_device(): pl.pallas_call(functools.partial(kernel, torus, slabs), out_shape=shapes,...]
where the time goes in v5:
time: 46.5 us; the launch traced here: 46.4 us
  Pallas kernels  44.5 us (96%)
  between operations  1.93 us (4%)
    pallas_call x1, Pallas kernels, per_device(): pl.pallas_call(functools.partial(kernel, torus, slabs), out_shape=shapes,...  43.7 us

profile of v5, /device:TPU:1, one launch (start us, length us, event | category | flops | bytes accessed | tf_op | source)
XLA Modules:
  0.0 46.4 jit_solution(12308057011798358858)
XLA Ops:
  1.9 43.7 %gated_level.1 = (f32[16,32,128]{2,1,0:T(8,128)S(1)}, f32[2,32,432]{2,1,0:T(8,128)S(1)}) custom-call(bf16[16,32,128]{2,1,0:T(8,128)(2,1)} %bitcast.6, bf16[16,32,128]{2,1,0:T(8,128)(2,1)} %bitcast.7, s32[2,32,128]{2,1,0:T(8,128)} %bitcast.8, f32[1]{0:T(128)S(6)} %copy.9.scale, s32[1]{0:T(128)S(6)} %copy.10.canary, bf16[2,32,432]{2,1,0:T(8,128)(2,1)} %ker_hbm.1), custom_call_target="tpu_custom_call" | custom-call | tf_op jit(solution)/shard_map/gated_level/pallas_call | solution.py:490
  45.6 0.8 %leave.1 = (f32[16,32,128]{2,1,0:T(8,128)}, f32[2,32,432]{2,1,0:T(8,128)}) custom-call(f32[16,32,128]{2,1,0:T(8,128)S(1)} %get-tuple-element.6.dx_in, f32[2,32,432]{2,1,0:T(8,128)S(1)} %get-tuple-element.7.kg_in), custom_call_target="tpu_custom_call" | custom-call | tf_op jit(solution)/shard_map/leave/pallas_call | solution.py:532
